TPU v7x, 32 devices: a whole 2x2x4 slice. The times are simulated.
32 devices in a mesh: ctx: 8 (over z, x), tp: 2 (over y), batch: 2 (over core).
Axes of the slice: x: 2, y: 2, z: 4, core: 2. Of those that a mesh axis runs over, the one named last changes fastest.
Arguments:
- queries: bfloat16 [4, 1024, 128, 128], P('batch', 'ctx', 'tp'), may hold values from -60 to 60, as said below
- span_key_rows: bfloat16 [4, 1024, 8, 128], P('batch', 'ctx', 'tp'), may hold values from -6 to 6
- span_value_rows: bfloat16 [4, 1024, 8, 128], P('batch', 'ctx', 'tp'), may hold values from -1.5 to 1.5
- prefix_key_rows: bfloat16 [4, 2048, 8, 128], P('batch', 'ctx', 'tp'), may hold values from -6 to 6
- prefix_value_rows: bfloat16 [4, 2048, 8, 128], P('batch', 'ctx', 'tp'), may hold values from -1.5 to 1.5
- cached_len: int32 [4], P('batch'), may hold values from 512 to 2048
- new_len: int32 [4], P('batch'), may hold values from 512 to 1024
- prefill_flag: int32 [4], P('batch'), may hold values from 0 to 1, as said below
- block_order: int32 [16], replicated, may hold values from 0 to 15, each once
Outputs:
- attended: bfloat16 [4, 1024, 128, 128], P('batch', 'ctx', 'tp')
Inputs may be any that keep to these rules, and one draw needn't show every extreme that they name: `queries`: large entries come in a few whole head vectors. `prefill_flag`: rows come in aligned pairs (rows 2k and 2k + 1): of each pair exactly one has the value 1.
All inputs are finite; a program needn't handle non-finite values.
Results may differ from a plain program's by a relative error of at most 0.012.
The roundings to bfloat16 on the way count: a program that leaves them out, or rounds other values in their place, can miss the bound.
Values may be sent and summed in bfloat16 or wider, within the bound.
No kernel may reach another device: no remote copies, remote signals or barrier semaphores. Data moves between devices by JAX's collectives and lax.ppermute only.
A program may use at most 320 MiB of HBM per device.

v0:
```python
import functools

import jax
import jax.numpy as jnp
from jax import lax
from jax.experimental import pallas as pl
from jax.experimental.pallas import tpu as pltpu
from jax.sharding import PartitionSpec as P


rope_base = 500000.0
neg_large = -1e30
log2e = 1.4426950408889634
streams = 2
far = 1 << 29


def ring_order(mesh):
    n = mesh.shape["ctx"]
    plain = list(range(n))
    choices = [
        plain[0::2] + plain[1::2][::-1],
        plain[: n // 2] + plain[n // 2 :][::-1],
        plain,
    ]
    axis = mesh.axis_names.index("ctx")
    line = mesh.devices
    for k in reversed(range(line.ndim)):
        if k != axis:
            line = line.take(0, axis=k)

    def length(order):
        total = 0
        for a, b in zip(order, order[1:] + order[:1]):
            ca, cb = (getattr(line[i], "coords", (i,)) for i in (a, b))
            total += sum(abs(u - v) for u, v in zip(ca, cb))
        return total

    return min(choices, key=length)


def rotate(x, cosine, sine):
    half = x.shape[-1] // 2
    wide = x.astype(jnp.float32)
    first = wide[..., :half]
    second = wide[..., half:]
    return jnp.concatenate(
        [first * cosine - second * sine, second * cosine + first * sine], -1
    ).astype(jnp.bfloat16)


def over_sublanes(op, x):
    for shift in (4, 2, 1):
        x = op(x, pltpu.roll(x, shift, 0))
    return x


def largest(s, top_ref):
    top_ref[...] = over_sublanes(jnp.maximum, jnp.max(s.reshape(-1, 8, s.shape[1]), axis=0))


def scores(q, k, s_ref, top_ref):
    s = lax.dot_general(k, q, (((1,), (1,)), ((), ())), preferred_element_type=jnp.float32)
    s_ref[...] = s
    largest(s, top_ref)


def absorb(tile, vt, s_ref, top_ref, m_ref, l_ref, acc_ref):
    size, width = acc_ref.shape[1:]
    factor = log2e / size**0.5
    before = m_ref[tile]
    top = jnp.maximum(before, top_ref[...])
    alpha = jnp.exp2((before - top) * factor)
    prob = jnp.exp2(s_ref[...].reshape(-1, 8, width) * factor - top * factor)
    l_ref[tile] = l_ref[tile] * alpha + jnp.sum(prob, axis=0)
    m_ref[tile] = top
    prob = prob.reshape(s_ref.shape).astype(jnp.bfloat16)
    acc = (acc_ref[tile].reshape(-1, 8, width) * alpha).reshape(size, width)
    acc_ref[tile] = acc + jnp.dot(vt, prob, preferred_element_type=jnp.float32)


def hide(bound, bases, s_ref, top_ref):
    run = s_ref.shape[0] // len(bases)
    tops = []
    for i, base in enumerate(bases):
        key = base + lax.broadcasted_iota(jnp.int32, (run, s_ref.shape[1]), 0)
        s = jnp.where(key <= bound, s_ref[i * run : (i + 1) * run], neg_large)
        s_ref[i * run : (i + 1) * run] = s
        tops.append(jnp.max(s.reshape(-1, 8, s.shape[1]), axis=0))
    top_ref[...] = over_sublanes(jnp.maximum, functools.reduce(jnp.maximum, tops))


def step_kernel(cfg, sc, q_ref, *refs):
    n, blocks, blk, first_head, sources, packed, fresh, last, chained = cfg
    refs = list(refs)
    take = lambda k: [refs.pop(0) for _ in range(k)]
    carry = [] if fresh else take(3)
    if packed:
        pairs = [(ref.at[0], ref.at[1]) for ref in take(len(sources))]
    else:
        pairs = [tuple(take(2))]
    if chained:
        take(1)
    if last:
        (o_ref,) = take(1)
        acc_ref, m_ref, l_ref = refs[-3:]
        stage, o_sem = refs[-5:-3]
    else:
        acc_ref, m_ref, l_ref = take(3)
    kbuf, vt_ref, s0, s1, t0, t1, work = take(7)
    rows, count, _, size = q_ref.shape
    heads = pairs[0][0].shape[0]
    width = acc_ref.shape[2]
    group = width // blk
    per = blocks // n
    tiles = rows * per
    local = pairs[0][0].shape[1] - rows * count
    chunk = s0.shape[0]
    slots = kbuf.shape[0] // heads
    runs = chunk // blk
    order = 4 + n

    bases = []
    for h in range(heads):
        slot = h * slots
        for k_ref, v_ref in pairs:
            for c in range(local // chunk):
                kbuf[slot] = k_ref[h, c * chunk : (c + 1) * chunk]
                vt_ref[slot] = v_ref[h, c * chunk : (c + 1) * chunk].T
                slot += 1
        for r in range(rows):
            at = slice(local + r * count, local + (r + 1) * count)
            keys = [k_ref[h, at] for k_ref, _ in pairs]
            values = [v_ref[h, at] for _, v_ref in pairs]
            if len(pairs) * count < chunk:
                rest = jnp.zeros((chunk - len(pairs) * count, size), keys[0].dtype)
                keys.append(rest)
                values.append(rest)
            kbuf[slot] = jnp.concatenate(keys, 0)
            vt_ref[slot] = jnp.concatenate(values, 0).T
            slot += 1
    for i in sources:
        for c in range(local // chunk):
            bases.append([sc[4 + i] * local + c * chunk + run * blk for run in range(runs)])
    fresh_bases = [
        sc[order + sc[4 + i] * per + b] * blk for i in sources for b in range(per)
    ]
    fresh_bases += [jnp.int32(far)] * (runs - len(fresh_bases))
    bases += [fresh_bases] * rows
    for slot, base in enumerate(bases):
        for run in range(runs):
            work[5 + run, slot] = base[run]

    if fresh:
        acc_ref[...] = jnp.zeros_like(acc_ref)
        m_ref[...] = jnp.full_like(m_ref, neg_large)
        l_ref[...] = jnp.zeros_like(l_ref)
    else:
        acc_ref[...] = carry[0][...]
        m_ref[...] = carry[1][...]
        l_ref[...] = carry[2][...]

    def put(at, go, tile, slot, mask, first, limit):
        work[0, at] = tile
        work[1, at] = slot
        work[2, at] = mask.astype(jnp.int32)
        work[3, at] = first
        work[4, at] = limit
        return at + go.astype(jnp.int32)

    total = jnp.int32(0)
    for h in range(heads):
        for r in range(rows):
            live = sc[2 + r]
            for b in range(per):
                tile = (h * rows + r) * per + b
                first = sc[order + sc[4] * per + b] * blk
                alive = first < live
                for slot, base in enumerate(bases):
                    place = slot - (len(bases) - rows)
                    if place >= 0 and place != r:
                        continue
                    low = functools.reduce(jnp.minimum, base)
                    high = functools.reduce(jnp.maximum, base) + blk - 1
                    if place >= 0:
                        limit = live - 1
                        seen = low <= jnp.minimum(first + blk - 1, limit)
                        mask = high > jnp.minimum(first, limit)
                        total = put(total, alive & seen, tile, h * slots + slot, mask, first, limit)
                    else:
                        limit = sc[1] - 1
                        go = alive & (sc[0] == r) & (low <= limit)
                        total = put(total, go, tile, h * slots + slot, high > limit, jnp.int32(far), limit)
    work[0, total] = work[0, jnp.maximum(total - 1, 0)]
    for extra in range(2):
        if extra:
            work[0, total + extra] = 0
        work[1, total + extra] = 0
        work[2, total + extra] = 1
        work[3, total + extra] = 0
        work[4, total + extra] = -1

    def prepare(at, s_ref, t_ref):
        tile = work[0, at]
        h, r, b = tile // tiles, (tile // per) % rows, tile % per
        heads_at = pl.ds(pl.multiple_of((first_head + h) * group, group), group)
        q = q_ref[r, pl.ds(b * blk, blk), heads_at, :].reshape(width, size)
        scores(q, kbuf[work[1, at]], s_ref, t_ref)

    def fix(at, s_ref, t_ref):
        @pl.when(work[2, at] == 1)
        def _():
            slot = work[1, at] % slots
            token = work[3, at] + lax.broadcasted_iota(jnp.int32, (1, width), 1) // group
            bound = jnp.minimum(token, work[4, at])
            hide(bound, [work[5 + run, slot] for run in range(runs)], s_ref, t_ref)

    def finish(at, s_ref, t_ref):
        absorb(work[0, at], vt_ref[work[1, at]], s_ref, t_ref, m_ref, l_ref, acc_ref)

    @pl.when(total > 0)
    def _():
        prepare(0, s0, t0)
        fix(0, s0, t0)

    def body(i, _):
        prepare(2 * i + 1, s1, t1)
        finish(2 * i, s0, t0)
        fix(2 * i + 1, s1, t1)
        prepare(2 * i + 2, s0, t0)
        finish(2 * i + 1, s1, t1)
        fix(2 * i + 2, s0, t0)
        return 0

    lax.fori_loop(0, (total + 1) // 2, body, 0)

    if last:

        def write(tile):
            h, r, b = tile // tiles, (tile // per) % rows, tile % per
            heads_at = pl.ds(pl.multiple_of((first_head + h) * group, group), group)
            return pltpu.make_async_copy(
                stage.at[tile], o_ref.at[r, pl.ds(b * blk, blk), heads_at], o_sem.at[tile]
            )

        def store(tile, _):
            r, b = (tile // per) % rows, tile % per
            first = sc[order + sc[4] * per + b] * blk
            live = sc[2 + r]

            @pl.when(first >= live)
            def _():
                stage[tile] = jnp.zeros(stage.shape[1:], stage.dtype)

            @pl.when(first < live)
            def _():
                sums = over_sublanes(jnp.add, l_ref[tile])
                out = (acc_ref[tile].reshape(-1, 8, width) / sums).reshape(size, width)
                query = lax.broadcasted_iota(jnp.int32, (1, width), 1)
                out = jnp.where(query < (live - first) * group, out, 0.0)
                stage[tile] = out.astype(stage.dtype).T.reshape(stage.shape[1:])

            write(tile).start()
            return 0

        lax.fori_loop(0, heads * tiles, store, 0)
        lax.fori_loop(0, heads * tiles, lambda t, _: (write(t).wait(), 0)[1], 0)


def step_call(scalars, q_rot, carry, parts, sources, out, last, first_head, blocks, n, group):
    rows, count, _, size = q_rot.shape
    packed = parts[0].ndim == 4
    unit_heads, depth, _ = parts[0].shape[-3:]
    local = depth - rows * count
    per = blocks // n
    blk = count // per
    width = blk * group
    tiles = unit_heads * rows * per
    chunk = 2 * count
    slots = len(sources) * (local // chunk) + rows
    items = unit_heads * rows * per * (slots - rows + 1) + 2
    fresh, chained = carry is None, last and out is not None
    vmem, anywhere = pl.BlockSpec(memory_space=pltpu.VMEM), pl.BlockSpec(memory_space=pl.ANY)
    state = lambda d: (tiles, d, width)
    f32 = lambda d: jax.ShapeDtypeStruct(state(d), jnp.float32)
    scratch = [
        pltpu.VMEM((unit_heads * slots, chunk, size), jnp.bfloat16),
        pltpu.VMEM((unit_heads * slots, size, chunk), jnp.bfloat16),
        pltpu.VMEM((chunk, width), jnp.float32),
        pltpu.VMEM((chunk, width), jnp.float32),
        pltpu.VMEM((8, width), jnp.float32),
        pltpu.VMEM((8, width), jnp.float32),
        pltpu.SMEM((5 + chunk // blk, max(items, slots)), jnp.int32),
    ]
    operands = [scalars, q_rot] + ([] if fresh else list(carry)) + list(parts)
    specs = [pl.BlockSpec(memory_space=pltpu.SMEM)] + [vmem] * (len(operands) - 1)
    aliases = {} if fresh or last else {2: 0, 3: 1, 4: 2}
    if last:
        scratch += [
            pltpu.VMEM((tiles, blk, group, size), jnp.bfloat16),
            pltpu.SemaphoreType.DMA((tiles,)),
        ] + [pltpu.VMEM(state(d), jnp.float32) for d in (size, 8, 8)]
        if chained:
            operands.append(out)
            specs.append(anywhere)
            aliases = {len(operands) - 1: 0}
        shapes, out_specs = jax.ShapeDtypeStruct(q_rot.shape, q_rot.dtype), anywhere
    else:
        shapes, out_specs = [f32(size), f32(8), f32(8)], [vmem] * 3
    cfg = (n, blocks, blk, first_head, tuple(sources), packed, fresh, last, chained)
    pairs = items * chunk * width
    return pl.pallas_call(
        functools.partial(step_kernel, cfg),
        in_specs=specs,
        out_specs=out_specs,
        scratch_shapes=scratch,
        out_shape=shapes,
        input_output_aliases=aliases,
        compiler_params=pltpu.CompilerParams(vmem_limit_bytes=24 * 1024 * 1024),
        cost_estimate=pl.CostEstimate(
            flops=pairs * size * 4, bytes_accessed=1024 * 1024, transcendentals=pairs
        ),
    )(*operands)


def turn_kernel(parts, q_ref, cosine_ref, sine_ref, o_ref):
    i = pl.program_id(0)
    tokens, _, size = q_ref.shape[1:]
    x = q_ref[0].astype(jnp.float32)
    cosine = cosine_ref[0][:, None, :]
    sine = sine_ref[0][:, None, :]
    turned = x * cosine + pltpu.roll(x, size // 2, 2) * sine
    at = pl.ds(pl.multiple_of((i % parts) * tokens, tokens), tokens)
    o_ref[i // parts, at] = turned.astype(o_ref.dtype)


def turn_call(queries, cosine, sine):
    rows, count, heads, size = queries.shape
    tokens = 16
    parts = count // tokens
    table = pl.BlockSpec((1, tokens, size), lambda i: (i // parts, i % parts, 0))
    return pl.pallas_call(
        functools.partial(turn_kernel, parts),
        grid=(rows * parts,),
        in_specs=[
            pl.BlockSpec((1, tokens, heads, size), lambda i: (i // parts, i % parts, 0, 0)),
            table,
            table,
        ],
        out_specs=pl.BlockSpec(queries.shape, lambda i: (0, 0, 0, 0)),
        out_shape=jax.ShapeDtypeStruct(queries.shape, queries.dtype),
        compiler_params=pltpu.CompilerParams(vmem_limit_bytes=16 * 1024 * 1024),
        cost_estimate=pl.CostEstimate(
            flops=queries.size * 4, bytes_accessed=queries.size * 4, transcendentals=0
        ),
        name="turn",
    )(queries, cosine, sine)


def shards(
    ring,
    queries,
    span_key_rows,
    span_value_rows,
    prefix_key_rows,
    prefix_value_rows,
    cached_len,
    new_len,
    prefill_flag,
    block_order,
):
    n = len(ring)
    rows, count, heads, size = queries.shape
    kv_heads = span_key_rows.shape[2]
    group = heads // kv_heads
    blocks = block_order.shape[0]
    per = blocks // n
    blk = count // per
    ctx = lax.axis_index("ctx")

    partial = jnp.where(prefill_flag[0] == 0, 0, 1).astype(jnp.int32)
    half = size // 2
    mine = lax.dynamic_slice(block_order, (ctx * per,), (per,))
    q_index = (mine[:, None] * blk + jnp.arange(blk, dtype=jnp.int32)[None, :]).reshape(count)
    base = jnp.where(prefill_flag == 1, 0, cached_len)
    positions = base[:, None] + q_index[None, :]
    inverse = rope_base ** (-(jnp.arange(half, dtype=jnp.float32) * 2.0 / size))
    angle = positions.astype(jnp.float32)[:, :, None, None] * inverse
    cosine = jnp.cos(angle)
    sine = jnp.sin(angle)
    unit = -(-kv_heads // streams)

    def payload(at):
        pick = lambda x: jnp.swapaxes(jnp.where(partial == 0, x[0], x[1])[:, at], 0, 1)
        new = lambda x: jnp.moveaxis(x, 2, 0).reshape(x.shape[2], rows * count, size)
        keys = new(rotate(span_key_rows[:, :, at], cosine, sine))
        values = new(span_value_rows[:, :, at])
        return jnp.stack(
            [
                jnp.concatenate([pick(prefix_key_rows), keys], 1),
                jnp.concatenate([pick(prefix_value_rows), values], 1),
            ]
        )

    both = lambda x, y: jnp.concatenate([x[:, :, 0], y[:, :, 0]], -1)
    q_rot = turn_call(queries, both(cosine, cosine), both(-sine, sine))

    place = {c: i for i, c in enumerate(ring)}
    table = jnp.array(
        [[ring[(place[c] - s) % n] for s in range(n)] for c in range(n)], jnp.int32
    )
    sources = lax.dynamic_slice(table, (ctx, 0), (1, n)).reshape(n)
    live = jnp.where(partial == 0, cached_len[0], cached_len[1])
    scalars = jnp.concatenate([partial[None], live[None], new_len, sources, block_order])

    forward = [(ring[i], ring[(i + 1) % n]) for i in range(n)]
    backward = [(b, a) for a, b in forward]

    def send(x, way):
        return lax.ppermute(x, "ctx", way)

    firsts = list(range(0, kv_heads, unit))
    count_u = len(firsts)
    own = [payload(slice(h, h + unit)) for h in firsts]
    ahead, back, carry = list(own), list(own), [None] * count_u
    out = None

    def step(todo, tied=None, last=False):
        u, parts, sources = todo
        return step_call(
            scalars if tied is None else tied,
            q_rot,
            carry[u],
            parts,
            sources,
            out,
            last,
            firsts[u],
            blocks,
            n,
            group,
        )

    for u in range(count_u):
        ahead[u], back[u] = send(ahead[u], forward), send(back[u], backward)
    carry[0] = step((0, [own[0]], [0]))
    waiting = [(u, [own[u]], [0]) for u in range(1, count_u)]
    for s in range(1, n // 2):
        for u in range(count_u):
            here, there, tied = lax.optimization_barrier((ahead[u], back[u], scalars))
            waiting.append((u, [here, there], [s, n - s]))
            if s + 1 == n // 2:
                here, there = here[0], there[1]
            if carry[u] is not None:
                here, there, carry[u] = lax.optimization_barrier((here, there, carry[u]))
            ahead[u], back[u] = send(here, forward), send(there, backward)
            todo = waiting.pop(0)
            carry[todo[0]] = step(todo, tied)
    for todo in waiting:
        carry[todo[0]] = step(todo)
    for u in range(count_u):
        out = step((u, [ahead[u], back[u]], [n // 2]), last=True)
    return out


def solution(mesh):
    ring = ring_order(mesh)
    return jax.shard_map(
        functools.partial(shards, ring),
        mesh=mesh,
        in_specs=(
            P("batch", "ctx", "tp", None),
            P("batch", "ctx", "tp", None),
            P("batch", "ctx", "tp", None),
            P("batch", "ctx", "tp", None),
            P("batch", "ctx", "tp", None),
            P("batch"),
            P("batch"),
            P("batch"),
            P(),
        ),
        out_specs=P("batch", "ctx", "tp", None),
        check_vma=False,
    )
```

profile of v0, /device:TPU:12, one launch (start us, length us, event | category | flops | bytes accessed | tf_op | source)
XLA Modules:
  0.0 124.5 jit_solution(1279222898513757760)
XLA Ops:
  6.8 1.6 %collective-permute-start.2 = (bf16[2,2,512,128]{3,2,1,0:T(8,128)(2,1)S(1)}, bf16[2,2,512,128]{3,2,1,0:T(8,128)(2,1)S(1)}, u32[]{:S(2)}, u32[]{:S(2)}) collective-permute-start(bf16[2,2,512,128]{3,2,1,0:T(8,128)(2,1)S(1)} %pad_maximum_fusion.1.refs_0_), channel_id=1, source_target_pairs={{0,8},{8,16},{16,24},{24,28},{28,20},{20,12},{12,4},{4,0},{1,9},{9... | collective-permute-start | bytes 1572872 | tf_op jit(solution)/shard_map/ppermute | solution.py:420
  9.0 1.6 %collective-permute-start = (bf16[2,2,512,128]{3,2,1,0:T(8,128)(2,1)S(1)}, bf16[2,2,512,128]{3,2,1,0:T(8,128)(2,1)S(1)}, u32[]{:S(2)}, u32[]{:S(2)}) collective-permute-start(bf16[2,2,512,128]{3,2,1,0:T(8,128)(2,1)S(1)} %pad_maximum_fusion.refs_0_), channel_id=1, source_target_pairs={{0,8},{8,16},{16,24},{24,28},{28,20},{20,12},{12,4},{4,0},{1,9},{9... | collective-permute-start | bytes 1572872 | tf_op jit(solution)/shard_map/ppermute | solution.py:420
  13.8 2.2 %copy-done = bf16[2,128,64,128]{3,2,1,0:T(8,128)(2,1)S(1)} copy-done((bf16[2,128,64,128]{3,2,1,0:T(8,128)(2,1)S(1)}, bf16[2,128,64,128]{3,2,1,0:T(8,128)(2,1)}, u32[]{:S(2)}) %copy-start) | copy-done | bytes 4194328
  16.0 2.6 %turn.1.q_ref = bf16[2,128,64,128]{3,2,1,0:T(8,128)(2,1)S(1)} custom-call(bf16[2,128,64,128]{3,2,1,0:T(8,128)(2,1)S(1)} %copy-done, f32[2,128,128]{2,1,0:T(8,128)S(1)} %get-tuple-element.174.cosine_ref, f32[2,128,128]{2,1,0:T(8,128)S(1)} %get-tuple-element.175.sine_ref), custom_call_target="tpu_custom_call" | custom-call | flops 8388608 | bytes 8388608 | tf_op jit(solution)/shard_map/turn/pallas_call | solution.py:342
  18.6 6.0 %shard_map.101 = (f32[8,128,1024]{2,1,0:T(8,128)S(1)}, f32[8,8,1024]{2,1,0:T(8,128)S(1)}, f32[8,8,1024]{2,1,0:T(8,128)S(1)}) custom-call(s32[28]{0:T(128)S(1)} %concatenate.29.sc, bf16[2,128,64,128]{3,2,1,0:T(8,128)(2,1)S(1)} %turn.1.q_ref, bf16[2,2,512,128]{3,2,1,0:T(8,128)(2,1)S(1)} %pad_maximum_fusion.1.refs_0_), custom_call_target="tpu_custom_call" | custom-call | flops 2415919104 | bytes 1048576 | tf_op jit(solution)/shard_map/pallas_call | solution.py:312
  24.7 7.0 %collective-permute-done.refs_3_ = bf16[2,2,512,128]{3,2,1,0:T(8,128)(2,1)S(1)} collective-permute-done((bf16[2,2,512,128]{3,2,1,0:T(8,128)(2,1)S(1)}, bf16[2,2,512,128]{3,2,1,0:T(8,128)(2,1)S(1)}, u32[]{:S(2)}, u32[]{:S(2)}) %collective-permute-start) | collective-permute-done | bytes 524320 | tf_op jit(solution)/shard_map/ppermute | solution.py:420
  33.0 1.6 %collective-permute-start.6 = (bf16[2,2,512,128]{3,2,1,0:T(8,128)(2,1)S(1)}, bf16[2,2,512,128]{3,2,1,0:T(8,128)(2,1)S(1)}, u32[]{:S(2)}, u32[]{:S(2)}) collective-permute-start(bf16[2,2,512,128]{3,2,1,0:T(8,128)(2,1)S(1)} %collective-permute-done.2.refs_3_), channel_id=1, source_target_pairs={{0,8},{8,16},{16,24},{24,28},{28,20},{20,12},{12,4},{4,0},{1,9},{9... | collective-permute-start | bytes 1572872 | tf_op jit(solution)/shard_map/ppermute | solution.py:420
  35.0 6.0 %shard_map.100 = (f32[8,128,1024]{2,1,0:T(8,128)S(1)}, f32[8,8,1024]{2,1,0:T(8,128)S(1)}, f32[8,8,1024]{2,1,0:T(8,128)S(1)}) custom-call(s32[28]{0:T(128)S(1)} %concatenate.29.sc, bf16[2,128,64,128]{3,2,1,0:T(8,128)(2,1)S(1)} %turn.1.q_ref, bf16[2,2,512,128]{3,2,1,0:T(8,128)(2,1)S(1)} %pad_maximum_fusion.refs_0_), custom_call_target="tpu_custom_call" | custom-call | flops 2415919104 | bytes 1048576 | tf_op jit(solution)/shard_map/pallas_call | solution.py:312
  41.1 1.6 %collective-permute-start.4 = (bf16[2,2,512,128]{3,2,1,0:T(8,128)(2,1)S(1)}, bf16[2,2,512,128]{3,2,1,0:T(8,128)(2,1)S(1)}, u32[]{:S(2)}, u32[]{:S(2)}) collective-permute-start(bf16[2,2,512,128]{3,2,1,0:T(8,128)(2,1)S(1)} %collective-permute-done.refs_3_), channel_id=1, source_target_pairs={{0,8},{8,16},{16,24},{24,28},{28,20},{20,12},{12,4},{4,0},{1,9},{9... | collective-permute-start | bytes 1572872 | tf_op jit(solution)/shard_map/ppermute | solution.py:420
  43.5 7.4 %shard_map.103 = (f32[8,128,1024]{2,1,0:T(8,128)S(1)}, f32[8,8,1024]{2,1,0:T(8,128)S(1)}, f32[8,8,1024]{2,1,0:T(8,128)S(1)}) custom-call(s32[28]{0:T(128)S(1)} %concatenate.29.sc, bf16[2,128,64,128]{3,2,1,0:T(8,128)(2,1)S(1)} %turn.1.q_ref, ...), custom_call_target="tpu_custom_call", output_to_operand_aliasing={{0}: (2, {}), {1}: (3, {}), {2}: (4, {})} | custom-call | flops 3489660928 | bytes 1048576 | tf_op jit(solution)/shard_map/pallas_call | solution.py:312
  50.8 5.9 %collective-permute-done.4.refs_3_ = bf16[2,2,512,128]{3,2,1,0:T(8,128)(2,1)S(1)} collective-permute-done((bf16[2,2,512,128]{3,2,1,0:T(8,128)(2,1)S(1)}, bf16[2,2,512,128]{3,2,1,0:T(8,128)(2,1)S(1)}, u32[]{:S(2)}, u32[]{:S(2)}) %collective-permute-start.4) | collective-permute-done | bytes 524320 | tf_op jit(solution)/shard_map/ppermute | solution.py:420
  58.1 1.5 %collective-permute-start.10 = (bf16[2,2,512,128]{3,2,1,0:T(8,128)(2,1)S(1)}, bf16[2,2,512,128]{3,2,1,0:T(8,128)(2,1)S(1)}, u32[]{:S(2)}, u32[]{:S(2)}) collective-permute-start(bf16[2,2,512,128]{3,2,1,0:T(8,128)(2,1)S(1)} %collective-permute-done.6.refs_3_), channel_id=1, source_target_pairs={{0,8},{8,16},{16,24},{24,28},{28,20},{20,12},{12,4},{4,0},{1,9},{9... | collective-permute-start | bytes 1572872 | tf_op jit(solution)/shard_map/ppermute | solution.py:420
  60.1 7.4 %shard_map.102 = (f32[8,128,1024]{2,1,0:T(8,128)S(1)}, f32[8,8,1024]{2,1,0:T(8,128)S(1)}, f32[8,8,1024]{2,1,0:T(8,128)S(1)}) custom-call(s32[28]{0:T(128)S(1)} %concatenate.29.sc, bf16[2,128,64,128]{3,2,1,0:T(8,128)(2,1)S(1)} %turn.1.q_ref, ...), custom_call_target="tpu_custom_call", output_to_operand_aliasing={{0}: (2, {}), {1}: (3, {}), {2}: (4, {})} | custom-call | flops 3489660928 | bytes 1048576 | tf_op jit(solution)/shard_map/pallas_call | solution.py:312
  67.5 2.0 %collective-permute-start.9 = (bf16[2,2,512,128]{3,2,1,0:T(8,128)(2,1)S(1)}, bf16[2,2,512,128]{3,2,1,0:T(8,128)(2,1)S(1)}, u32[]{:S(2)}, u32[]{:S(2)}) collective-permute-start(bf16[2,2,512,128]{3,2,1,0:T(8,128)(2,1)S(1)} %collective-permute-done.5.refs_4_), channel_id=1, source_target_pairs={{8,0},{16,8},{24,16},{28,24},{20,28},{12,20},{4,12},{0,4},{9,1},{1... | collective-permute-start | bytes 1572872 | tf_op jit(solution)/shard_map/ppermute | solution.py:420
  69.5 8.3 %shard_map.106 = (f32[8,128,1024]{2,1,0:T(8,128)S(1)}, f32[8,8,1024]{2,1,0:T(8,128)S(1)}, f32[8,8,1024]{2,1,0:T(8,128)S(1)}) custom-call(s32[28]{0:T(128)S(1)} %concatenate.29.sc, bf16[2,128,64,128]{3,2,1,0:T(8,128)(2,1)S(1)} %turn.1.q_ref, ...), custom_call_target="tpu_custom_call", output_to_operand_aliasing={{0}: (2, {}), {1}: (3, {}), {2}: (4, {})} | custom-call | flops 3489660928 | bytes 1048576 | tf_op jit(solution)/shard_map/pallas_call | solution.py:312
  77.9 2.8 %collective-permute-done.8.refs_3_ = bf16[2,2,512,128]{3,2,1,0:T(8,128)(2,1)S(1)} collective-permute-done((bf16[2,2,512,128]{3,2,1,0:T(8,128)(2,1)S(1)}, bf16[2,2,512,128]{3,2,1,0:T(8,128)(2,1)S(1)}, u32[]{:S(2)}, u32[]{:S(2)}) %collective-permute-start.8) | collective-permute-done | bytes 524320 | tf_op jit(solution)/shard_map/ppermute | solution.py:420
  80.7 1.7 %collective-permute-done.9.refs_4_ = bf16[2,2,512,128]{3,2,1,0:T(8,128)(2,1)S(1)} collective-permute-done((bf16[2,2,512,128]{3,2,1,0:T(8,128)(2,1)S(1)}, bf16[2,2,512,128]{3,2,1,0:T(8,128)(2,1)S(1)}, u32[]{:S(2)}, u32[]{:S(2)}) %collective-permute-start.9) | collective-permute-done | bytes 524320 | tf_op jit(solution)/shard_map/ppermute | solution.py:420
  82.7 1.7 %collective-permute-start.15 = (bf16[2,512,128]{2,1,0:T(8,128)(2,1)S(1)}, bf16[2,512,128]{2,1,0:T(8,128)(2,1)S(1)}, u32[]{:S(2)}, u32[]{:S(2)}) collective-permute-start(bf16[2,512,128]{2,1,0:T(8,128)(2,1)S(1)} %slice_bitcast_fusion), channel_id=1, source_target_pairs={{8,0},{16,8},{24,16},{28,24},{20,28},{12,20},{4,12},{0,4},{9,1},{1... | collective-permute-start | bytes 786440 | tf_op jit(solution)/shard_map/ppermute | solution.py:420
  84.5 8.3 %shard_map.104 = (f32[8,128,1024]{2,1,0:T(8,128)S(1)}, f32[8,8,1024]{2,1,0:T(8,128)S(1)}, f32[8,8,1024]{2,1,0:T(8,128)S(1)}) custom-call(s32[28]{0:T(128)S(1)} %concatenate.29.sc, bf16[2,128,64,128]{3,2,1,0:T(8,128)(2,1)S(1)} %turn.1.q_ref, ...), custom_call_target="tpu_custom_call", output_to_operand_aliasing={{0}: (2, {}), {1}: (3, {}), {2}: (4, {})} | custom-call | flops 3489660928 | bytes 1048576 | tf_op jit(solution)/shard_map/pallas_call | solution.py:312
  93.1 1.7 %collective-permute-start.13 = (bf16[2,512,128]{2,1,0:T(8,128)(2,1)S(1)}, bf16[2,512,128]{2,1,0:T(8,128)(2,1)S(1)}, u32[]{:S(2)}, u32[]{:S(2)}) collective-permute-start(bf16[2,512,128]{2,1,0:T(8,128)(2,1)S(1)} %slice_bitcast_fusion.2), channel_id=1, source_target_pairs={{8,0},{16,8},{24,16},{28,24},{20,28},{12,20},{4,12},{0,4},{9,1},{1... | collective-permute-start | bytes 786440 | tf_op jit(solution)/shard_map/ppermute | solution.py:420
  94.9 6.5 %shard_map.105 = (f32[8,128,1024]{2,1,0:T(8,128)S(1)}, f32[8,8,1024]{2,1,0:T(8,128)S(1)}, f32[8,8,1024]{2,1,0:T(8,128)S(1)}) custom-call(s32[28]{0:T(128)S(1)} %concatenate.29.sc, bf16[2,128,64,128]{3,2,1,0:T(8,128)(2,1)S(1)} %turn.1.q_ref, ...), custom_call_target="tpu_custom_call", output_to_operand_aliasing={{0}: (2, {}), {1}: (3, {}), {2}: (4, {})} | custom-call | flops 3489660928 | bytes 1048576 | tf_op jit(solution)/shard_map/pallas_call | solution.py:312
  101.4 6.7 %shard_map.107 = (f32[8,128,1024]{2,1,0:T(8,128)S(1)}, f32[8,8,1024]{2,1,0:T(8,128)S(1)}, f32[8,8,1024]{2,1,0:T(8,128)S(1)}) custom-call(s32[28]{0:T(128)S(1)} %concatenate.29.sc, bf16[2,128,64,128]{3,2,1,0:T(8,128)(2,1)S(1)} %turn.1.q_ref, ...), custom_call_target="tpu_custom_call", output_to_operand_aliasing={{0}: (2, {}), {1}: (3, {}), {2}: (4, {})} | custom-call | flops 3489660928 | bytes 1048576 | tf_op jit(solution)/shard_map/pallas_call | solution.py:312
  108.1 8.1 %shard_map.108.refs_5_ = bf16[2,128,64,128]{3,2,1,0:T(8,128)(2,1)} custom-call(s32[28]{0:T(128)S(1)} %concatenate.29.sc, bf16[2,128,64,128]{3,2,1,0:T(8,128)(2,1)S(1)} %turn.1.q_ref, f32[8,128,1024]{2,1,0:T(8,128)S(1)} %get-tuple-element.144.refs_0_, f32[8,8,1024]{2,1,0:T(8,128)S(1)} %get-tuple-element.145.refs_1_, ...), custom_call_target="tpu_custom_call" | custom-call | flops 2415919104 | bytes 1048576 | tf_op jit(solution)/shard_map/pallas_call | solution.py:312
  116.2 8.1 %shard_map.109 = bf16[2,128,64,128]{3,2,1,0:T(8,128)(2,1)} custom-call(s32[28]{0:T(128)S(1)} %concatenate.29.sc, bf16[2,128,64,128]{3,2,1,0:T(8,128)(2,1)S(1)} %turn.1.q_ref, f32[8,128,1024]{2,1,0:T(8,128)S(1)} %get-tuple-element.126.refs_0_, f32[8,8,1024]{2,1,0:T(8,128)S(1)} %get-tuple-element.127.refs_1_, ...), custom_call_target="tpu_custom_call", output_to_operand_aliasing={{}: (7, {})} | custom-call | flops 2415919104 | bytes 1048576 | tf_op jit(solution)/shard_map/pallas_call | solution.py:312
  (67 shorter events, 13.6 us)
Async XLA Ops:
  0.0 5.8 %copy-start.1 = (bf16[2,256,4,128]{3,2,1,0:T(4,128)(2,1)S(1)}, bf16[2,256,4,128]{3,2,1,0:T(4,128)(2,1)}, u32[]{:S(2)}) copy-start(bf16[2,256,4,128]{3,2,1,0:T(4,128)(2,1)} %param.13) | copy-start | bytes 1572868
  0.0 6.0 %copy-start.2 = (bf16[2,256,4,128]{3,2,1,0:T(4,128)(2,1)S(1)}, bf16[2,256,4,128]{3,2,1,0:T(4,128)(2,1)}, u32[]{:S(2)}) copy-start(bf16[2,256,4,128]{3,2,1,0:T(4,128)(2,1)} %param.14) | copy-start | bytes 1572868
  2.2 4.2 %copy-start.3 = (bf16[2,128,4,128]{3,2,1,0:T(4,128)(2,1)S(1)}, bf16[2,128,4,128]{3,2,1,0:T(4,128)(2,1)}, u32[]{:S(2)}) copy-start(bf16[2,128,4,128]{3,2,1,0:T(4,128)(2,1)} %param.12) | copy-start | bytes 786436
  6.2 4.9 %copy-start.4 = (s32[2]{0:T(128)S(1)}, s32[2]{0:T(128)}, u32[]{:S(2)}) copy-start(s32[2]{0:T(128)} %param.15) | copy-start | bytes 28
  6.2 7.4 %copy-start.5 = (s32[2]{0:T(128)S(1)}, s32[2]{0:T(128)}, u32[]{:S(2)}) copy-start(s32[2]{0:T(128)} %param.16) | copy-start | bytes 28
  6.2 7.4 %copy-start.6 = (s32[16]{0:T(128)S(1)}, s32[16]{0:T(128)}, u32[]{:S(2)}) copy-start(s32[16]{0:T(128)} %param.18) | copy-start | bytes 196
  6.8 17.9 %collective-permute-start.2 = (bf16[2,2,512,128]{3,2,1,0:T(8,128)(2,1)S(1)}, bf16[2,2,512,128]{3,2,1,0:T(8,128)(2,1)S(1)}, u32[]{:S(2)}, u32[]{:S(2)}) collective-permute-start(bf16[2,2,512,128]{3,2,1,0:T(8,128)(2,1)S(1)} %pad_maximum_fusion.1.refs_0_), channel_id=1, source_target_pairs={{0,8},{8,16},{16,24},{24,28},{28,20},{20,12},{12,4},{4,0},{1,9},{9... | collective-permute-start | bytes 1572872 | tf_op jit(solution)/shard_map/ppermute | solution.py:420
  8.4 16.3 %collective-permute-start.3 = (bf16[2,2,512,128]{3,2,1,0:T(8,128)(2,1)S(1)}, bf16[2,2,512,128]{3,2,1,0:T(8,128)(2,1)S(1)}, u32[]{:S(2)}, u32[]{:S(2)}) collective-permute-start(bf16[2,2,512,128]{3,2,1,0:T(8,128)(2,1)S(1)} %pad_maximum_fusion.1.refs_0_), channel_id=1, source_target_pairs={{8,0},{16,8},{24,16},{28,24},{20,28},{12,20},{4,12},{0,4},{9,1},{1... | collective-permute-start | bytes 1572872 | tf_op jit(solution)/shard_map/ppermute | solution.py:420
  9.0 22.7 %collective-permute-start = (bf16[2,2,512,128]{3,2,1,0:T(8,128)(2,1)S(1)}, bf16[2,2,512,128]{3,2,1,0:T(8,128)(2,1)S(1)}, u32[]{:S(2)}, u32[]{:S(2)}) collective-permute-start(bf16[2,2,512,128]{3,2,1,0:T(8,128)(2,1)S(1)} %pad_maximum_fusion.refs_0_), channel_id=1, source_target_pairs={{0,8},{8,16},{16,24},{24,28},{28,20},{20,12},{12,4},{4,0},{1,9},{9... | collective-permute-start | bytes 1572872 | tf_op jit(solution)/shard_map/ppermute | solution.py:420
  10.6 22.4 %collective-permute-start.1 = (bf16[2,2,512,128]{3,2,1,0:T(8,128)(2,1)S(1)}, bf16[2,2,512,128]{3,2,1,0:T(8,128)(2,1)S(1)}, u32[]{:S(2)}, u32[]{:S(2)}) collective-permute-start(bf16[2,2,512,128]{3,2,1,0:T(8,128)(2,1)S(1)} %pad_maximum_fusion.refs_0_), channel_id=1, source_target_pairs={{8,0},{16,8},{24,16},{28,24},{20,28},{12,20},{4,12},{0,4},{9,1},{1... | collective-permute-start | bytes 1572872 | tf_op jit(solution)/shard_map/ppermute | solution.py:420
  13.8 2.2 %copy-start = (bf16[2,128,64,128]{3,2,1,0:T(8,128)(2,1)S(1)}, bf16[2,128,64,128]{3,2,1,0:T(8,128)(2,1)}, u32[]{:S(2)}) copy-start(bf16[2,128,64,128]{3,2,1,0:T(8,128)(2,1)} %q_ref.1) | copy-start | bytes 12582916
  33.0 17.8 %collective-permute-start.6 = (bf16[2,2,512,128]{3,2,1,0:T(8,128)(2,1)S(1)}, bf16[2,2,512,128]{3,2,1,0:T(8,128)(2,1)S(1)}, u32[]{:S(2)}, u32[]{:S(2)}) collective-permute-start(bf16[2,2,512,128]{3,2,1,0:T(8,128)(2,1)S(1)} %collective-permute-done.2.refs_3_), channel_id=1, source_target_pairs={{0,8},{8,16},{16,24},{24,28},{28,20},{20,12},{12,4},{4,0},{1,9},{9... | collective-permute-start | bytes 1572872 | tf_op jit(solution)/shard_map/ppermute | solution.py:420
  34.6 16.3 %collective-permute-start.7 = (bf16[2,2,512,128]{3,2,1,0:T(8,128)(2,1)S(1)}, bf16[2,2,512,128]{3,2,1,0:T(8,128)(2,1)S(1)}, u32[]{:S(2)}, u32[]{:S(2)}) collective-permute-start(bf16[2,2,512,128]{3,2,1,0:T(8,128)(2,1)S(1)} %collective-permute-done.3.refs_4_), channel_id=1, source_target_pairs={{8,0},{16,8},{24,16},{28,24},{20,28},{12,20},{4,12},{0,4},{9,1},{1... | collective-permute-start | bytes 1572872 | tf_op jit(solution)/shard_map/ppermute | solution.py:420
  41.1 15.7 %collective-permute-start.4 = (bf16[2,2,512,128]{3,2,1,0:T(8,128)(2,1)S(1)}, bf16[2,2,512,128]{3,2,1,0:T(8,128)(2,1)S(1)}, u32[]{:S(2)}, u32[]{:S(2)}) collective-permute-start(bf16[2,2,512,128]{3,2,1,0:T(8,128)(2,1)S(1)} %collective-permute-done.refs_3_), channel_id=1, source_target_pairs={{0,8},{8,16},{16,24},{24,28},{28,20},{20,12},{12,4},{4,0},{1,9},{9... | collective-permute-start | bytes 1572872 | tf_op jit(solution)/shard_map/ppermute | solution.py:420
  42.7 15.4 %collective-permute-start.5 = (bf16[2,2,512,128]{3,2,1,0:T(8,128)(2,1)S(1)}, bf16[2,2,512,128]{3,2,1,0:T(8,128)(2,1)S(1)}, u32[]{:S(2)}, u32[]{:S(2)}) collective-permute-start(bf16[2,2,512,128]{3,2,1,0:T(8,128)(2,1)S(1)} %collective-permute-done.1.refs_4_), channel_id=1, source_target_pairs={{8,0},{16,8},{24,16},{28,24},{20,28},{12,20},{4,12},{0,4},{9,1},{1... | collective-permute-start | bytes 1572872 | tf_op jit(solution)/shard_map/ppermute | solution.py:420
  58.1 19.8 %collective-permute-start.10 = (bf16[2,2,512,128]{3,2,1,0:T(8,128)(2,1)S(1)}, bf16[2,2,512,128]{3,2,1,0:T(8,128)(2,1)S(1)}, u32[]{:S(2)}, u32[]{:S(2)}) collective-permute-start(bf16[2,2,512,128]{3,2,1,0:T(8,128)(2,1)S(1)} %collective-permute-done.6.refs_3_), channel_id=1, source_target_pairs={{0,8},{8,16},{16,24},{24,28},{28,20},{20,12},{12,4},{4,0},{1,9},{9... | collective-permute-start | bytes 1572872 | tf_op jit(solution)/shard_map/ppermute | solution.py:420
  59.6 18.3 %collective-permute-start.11 = (bf16[2,2,512,128]{3,2,1,0:T(8,128)(2,1)S(1)}, bf16[2,2,512,128]{3,2,1,0:T(8,128)(2,1)S(1)}, u32[]{:S(2)}, u32[]{:S(2)}) collective-permute-start(bf16[2,2,512,128]{3,2,1,0:T(8,128)(2,1)S(1)} %collective-permute-done.7.refs_4_), channel_id=1, source_target_pairs={{8,0},{16,8},{24,16},{28,24},{20,28},{12,20},{4,12},{0,4},{9,1},{1... | collective-permute-start | bytes 1572872 | tf_op jit(solution)/shard_map/ppermute | solution.py:420
  67.5 13.2 %collective-permute-start.8 = (bf16[2,2,512,128]{3,2,1,0:T(8,128)(2,1)S(1)}, bf16[2,2,512,128]{3,2,1,0:T(8,128)(2,1)S(1)}, u32[]{:S(2)}, u32[]{:S(2)}) collective-permute-start(bf16[2,2,512,128]{3,2,1,0:T(8,128)(2,1)S(1)} %collective-permute-done.4.refs_3_), channel_id=1, source_target_pairs={{0,8},{8,16},{16,24},{24,28},{28,20},{20,12},{12,4},{4,0},{1,9},{9... | collective-permute-start | bytes 1572872 | tf_op jit(solution)/shard_map/ppermute | solution.py:420
  67.5 14.9 %collective-permute-start.9 = (bf16[2,2,512,128]{3,2,1,0:T(8,128)(2,1)S(1)}, bf16[2,2,512,128]{3,2,1,0:T(8,128)(2,1)S(1)}, u32[]{:S(2)}, u32[]{:S(2)}) collective-permute-start(bf16[2,2,512,128]{3,2,1,0:T(8,128)(2,1)S(1)} %collective-permute-done.5.refs_4_), channel_id=1, source_target_pairs={{8,0},{16,8},{24,16},{28,24},{20,28},{12,20},{4,12},{0,4},{9,1},{1... | collective-permute-start | bytes 1572872 | tf_op jit(solution)/shard_map/ppermute | solution.py:420
  82.4 25.7 %collective-permute-start.14 = (bf16[2,512,128]{2,1,0:T(8,128)(2,1)S(1)}, bf16[2,512,128]{2,1,0:T(8,128)(2,1)S(1)}, u32[]{:S(2)}, u32[]{:S(2)}) collective-permute-start(bf16[2,512,128]{2,1,0:T(8,128)(2,1)S(1)} %slice_bitcast_fusion.1), channel_id=1, source_target_pairs={{0,8},{8,16},{16,24},{24,28},{28,20},{20,12},{12,4},{4,0},{1,9},{9... | collective-permute-start | bytes 786440 | tf_op jit(solution)/shard_map/ppermute | solution.py:420
  82.7 25.5 %collective-permute-start.15 = (bf16[2,512,128]{2,1,0:T(8,128)(2,1)S(1)}, bf16[2,512,128]{2,1,0:T(8,128)(2,1)S(1)}, u32[]{:S(2)}, u32[]{:S(2)}) collective-permute-start(bf16[2,512,128]{2,1,0:T(8,128)(2,1)S(1)} %slice_bitcast_fusion), channel_id=1, source_target_pairs={{8,0},{16,8},{24,16},{28,24},{20,28},{12,20},{4,12},{0,4},{9,1},{1... | collective-permute-start | bytes 786440 | tf_op jit(solution)/shard_map/ppermute | solution.py:420
  92.8 23.4 %collective-permute-start.12 = (bf16[2,512,128]{2,1,0:T(8,128)(2,1)S(1)}, bf16[2,512,128]{2,1,0:T(8,128)(2,1)S(1)}, u32[]{:S(2)}, u32[]{:S(2)}) collective-permute-start(bf16[2,512,128]{2,1,0:T(8,128)(2,1)S(1)} %slice_bitcast_fusion.3), channel_id=1, source_target_pairs={{0,8},{8,16},{16,24},{24,28},{28,20},{20,12},{12,4},{4,0},{1,9},{9... | collective-permute-start | bytes 786440 | tf_op jit(solution)/shard_map/ppermute | solution.py:420
  93.1 23.1 %collective-permute-start.13 = (bf16[2,512,128]{2,1,0:T(8,128)(2,1)S(1)}, bf16[2,512,128]{2,1,0:T(8,128)(2,1)S(1)}, u32[]{:S(2)}, u32[]{:S(2)}) collective-permute-start(bf16[2,512,128]{2,1,0:T(8,128)(2,1)S(1)} %slice_bitcast_fusion.2), channel_id=1, source_target_pairs={{8,0},{16,8},{24,16},{28,24},{20,28},{12,20},{4,12},{0,4},{9,1},{1... | collective-permute-start | bytes 786440 | tf_op jit(solution)/shard_map/ppermute | solution.py:420
where the time goes:
time: 125 us; the launch traced here: 124 us
  Pallas kernels  75.4 us (60%)
  waiting for transfers between devices  20 us (16%)
  starting transfers between devices  16.8 us (13%)
  other arithmetic  5.43 us (4%)
  local copies, waits for them, and re-layouts  4.41 us (4%)
  between operations  2.47 us (2%)
    pallas_call x10, Pallas kernels, step_call(): pl.pallas_call(functools.partial(step_kernel, cfg), in_specs=specs, out_s...  72.8 us
    ppermute x16, waiting for transfers between devices, send(): return lax.ppermute(x, 'ctx', way)  20 us
    ppermute x16, starting transfers between devices, send(): return lax.ppermute(x, 'ctx', way)  16.8 us
    pallas_call x1, Pallas kernels, turn_call(): pl.pallas_call(functools.partial(turn_kernel, parts), grid=(rows * parts,...  2.61 us
  transfers between devices with their start and end apart: 16, of which 6 were waited for; matrix products, arithmetic and copies ran while one was open for 1% of the time, Pallas kernels for 54%

commit v1 on v0

--- a/solution.py
+++ b/solution.py
@@ -12,6 +12,7 @@
 neg_large = -1e30
 log2e = 1.4426950408889634
 streams = 2
+chunk_units = 4
 far = 1 << 29
 
 
@@ -79,26 +80,47 @@
     acc_ref[tile] = acc + jnp.dot(vt, prob, preferred_element_type=jnp.float32)
 
 
-def hide(bound, bases, s_ref, top_ref):
-    run = s_ref.shape[0] // len(bases)
+def hide(token, runs, s_ref, top_ref):
+    size = s_ref.shape[0] // len(runs)
     tops = []
-    for i, base in enumerate(bases):
-        key = base + lax.broadcasted_iota(jnp.int32, (run, s_ref.shape[1]), 0)
-        s = jnp.where(key <= bound, s_ref[i * run : (i + 1) * run], neg_large)
-        s_ref[i * run : (i + 1) * run] = s
+    for i, (base, offset, limit) in enumerate(runs):
+        bound = jnp.minimum(token + offset, limit) - base
+        key = lax.broadcasted_iota(jnp.int32, (size, s_ref.shape[1]), 0)
+        s = jnp.where(key <= bound, s_ref[i * size : (i + 1) * size], neg_large)
+        s_ref[i * size : (i + 1) * size] = s
         tops.append(jnp.max(s.reshape(-1, 8, s.shape[1]), axis=0))
     top_ref[...] = over_sublanes(jnp.maximum, functools.reduce(jnp.maximum, tops))
 
 
+def plan(n, cache_units):
+    half = n // 2
+    steps, partial, prefill = [], [], []
+    for s in range(1, half + 1):
+        arrived = [s, n - s] if s < half else [half]
+        for source in ([0] if s == 1 else []) + arrived:
+            partial += [(source, c) for c in range(cache_units)] + [(source, None)]
+            prefill += [(source, None)]
+        chunks = []
+        for kind, queue in ((0, partial), (1, prefill)):
+            while len(queue) >= chunk_units or (s == half and queue):
+                chunks.append((kind, tuple(queue[:chunk_units])))
+                del queue[:chunk_units]
+        steps.append(chunks)
+    return steps
+
+
 def step_kernel(cfg, sc, q_ref, *refs):
-    n, blocks, blk, first_head, sources, packed, fresh, last, chained = cfg
+    n, blocks, blk, first_head, chunks, sources, packed, fresh, last, chained = cfg
     refs = list(refs)
     take = lambda k: [refs.pop(0) for _ in range(k)]
     carry = [] if fresh else take(3)
-    if packed:
-        pairs = [(ref.at[0], ref.at[1]) for ref in take(len(sources))]
-    else:
-        pairs = [tuple(take(2))]
+    pairs = {}
+    for source, one in zip(sources, packed):
+        if one:
+            (ref,) = take(1)
+            pairs[source] = (ref.at[0], ref.at[1])
+        else:
+            pairs[source] = tuple(take(2))
     if chained:
         take(1)
     if last:
@@ -107,49 +129,57 @@
         stage, o_sem = refs[-5:-3]
     else:
         acc_ref, m_ref, l_ref = take(3)
-    kbuf, vt_ref, s0, s1, t0, t1, work = take(7)
+    kbuf, vt_ref, qbuf, s0, s1, t0, t1, work, q_sem = take(9)
     rows, count, _, size = q_ref.shape
-    heads = pairs[0][0].shape[0]
+    heads = pairs[sources[0]][0].shape[0]
     width = acc_ref.shape[2]
     group = width // blk
     per = blocks // n
     tiles = rows * per
-    local = pairs[0][0].shape[1] - rows * count
-    chunk = s0.shape[0]
-    slots = kbuf.shape[0] // heads
-    runs = chunk // blk
+    local = pairs[sources[0]][0].shape[1] - rows * count
+    runs = s0.shape[0] // blk
     order = 4 + n
-
-    bases = []
-    for h in range(heads):
-        slot = h * slots
-        for k_ref, v_ref in pairs:
-            for c in range(local // chunk):
-                kbuf[slot] = k_ref[h, c * chunk : (c + 1) * chunk]
-                vt_ref[slot] = v_ref[h, c * chunk : (c + 1) * chunk].T
-                slot += 1
-        for r in range(rows):
-            at = slice(local + r * count, local + (r + 1) * count)
-            keys = [k_ref[h, at] for k_ref, _ in pairs]
-            values = [v_ref[h, at] for _, v_ref in pairs]
-            if len(pairs) * count < chunk:
-                rest = jnp.zeros((chunk - len(pairs) * count, size), keys[0].dtype)
-                keys.append(rest)
-                values.append(rest)
-            kbuf[slot] = jnp.concatenate(keys, 0)
-            vt_ref[slot] = jnp.concatenate(values, 0).T
-            slot += 1
-    for i in sources:
-        for c in range(local // chunk):
-            bases.append([sc[4 + i] * local + c * chunk + run * blk for run in range(runs)])
-    fresh_bases = [
-        sc[order + sc[4 + i] * per + b] * blk for i in sources for b in range(per)
-    ]
-    fresh_bases += [jnp.int32(far)] * (runs - len(fresh_bases))
-    bases += [fresh_bases] * rows
-    for slot, base in enumerate(bases):
-        for run in range(runs):
-            work[5 + run, slot] = base[run]
+    row_of = lambda kind: sc[0] if kind == 0 else 1 - sc[0]
+    run_at = 5
+
+    def fetch(tile):
+        h, r, b = tile // tiles, (tile // per) % rows, tile % per
+        heads_at = pl.ds((first_head + h) * group, group)
+        return pltpu.make_async_copy(
+            q_ref.at[r, pl.ds(b * blk, blk), heads_at], qbuf.at[tile], q_sem.at[tile]
+        )
+
+    for tile in range(heads * tiles):
+        fetch(tile).start()
+
+    for i, (kind, units) in enumerate(chunks):
+        row = row_of(kind)
+        live = sc[2 + row]
+        table = []
+        for h in range(heads):
+            keys, values = [], []
+            for source, c in units:
+                k_ref, v_ref = pairs[source]
+                start = local + row * count if c is None else c * count
+                at = pl.ds(start if c is not None else pl.multiple_of(start, count), count)
+                keys.append(k_ref[h, at])
+                values.append(v_ref[h, at])
+            rest = s0.shape[0] - len(units) * count
+            if rest:
+                keys.append(jnp.zeros((rest, size), keys[0].dtype))
+                values.append(jnp.zeros((rest, size), keys[0].dtype))
+            kbuf[h * len(chunks) + i] = jnp.concatenate(keys, 0)
+            vt_ref[h * len(chunks) + i] = jnp.concatenate(values, 0).T
+        for source, c in units:
+            for b in range(per):
+                if c is None:
+                    table.append((sc[order + sc[4 + source] * per + b] * blk, 0, live - 1))
+                else:
+                    table.append((sc[4 + source] * local + c * count + b * blk, far, sc[1] - 1))
+        table += [(0, 0, -1)] * (runs - len(table))
+        for run, entry in enumerate(table):
+            for j, value in enumerate(entry):
+                work[run_at + 3 * run + j, i] = value
 
     if fresh:
         acc_ref[...] = jnp.zeros_like(acc_ref)
@@ -160,63 +190,60 @@
         m_ref[...] = carry[1][...]
         l_ref[...] = carry[2][...]
 
-    def put(at, go, tile, slot, mask, first, limit):
-        work[0, at] = tile
-        work[1, at] = slot
-        work[2, at] = mask.astype(jnp.int32)
-        work[3, at] = first
-        work[4, at] = limit
-        return at + go.astype(jnp.int32)
-
     total = jnp.int32(0)
-    for h in range(heads):
-        for r in range(rows):
-            live = sc[2 + r]
-            for b in range(per):
-                tile = (h * rows + r) * per + b
-                first = sc[order + sc[4] * per + b] * blk
-                alive = first < live
-                for slot, base in enumerate(bases):
-                    place = slot - (len(bases) - rows)
-                    if place >= 0 and place != r:
-                        continue
-                    low = functools.reduce(jnp.minimum, base)
-                    high = functools.reduce(jnp.maximum, base) + blk - 1
-                    if place >= 0:
-                        limit = live - 1
-                        seen = low <= jnp.minimum(first + blk - 1, limit)
-                        mask = high > jnp.minimum(first, limit)
-                        total = put(total, alive & seen, tile, h * slots + slot, mask, first, limit)
-                    else:
-                        limit = sc[1] - 1
-                        go = alive & (sc[0] == r) & (low <= limit)
-                        total = put(total, go, tile, h * slots + slot, high > limit, jnp.int32(far), limit)
+    for i, (kind, _) in enumerate(chunks):
+        row = row_of(kind)
+        for b in range(per):
+            first = sc[order + sc[4] * per + b] * blk
+
+            def look(run, state, first=first, i=i):
+                seen, hidden = state
+                base, offset, limit = (work[run_at + 3 * run + j, i] for j in range(3))
+                least = jnp.minimum(first + offset, limit)
+                most = jnp.minimum(first + blk - 1 + offset, limit)
+                seen = seen | (base <= most).astype(jnp.int32)
+                return seen, hidden | (base + blk - 1 > least).astype(jnp.int32)
+
+            state = (jnp.int32(0), jnp.int32(0))
+            for run in range(runs):
+                state = look(run, state)
+            go = jnp.where(first < sc[2 + row], state[0], 0)
+            for h in range(heads):
+                work[0, total] = (h * rows + row) * per + b
+                work[1, total] = h * len(chunks) + i
+                work[2, total] = state[1]
+                work[3, total] = first
+                work[4, total] = i
+                total = total + go
+    none = len(chunks)
+    for run in range(runs):
+        for j, value in enumerate((0, 0, -1)):
+            work[run_at + 3 * run + j, none] = value
     work[0, total] = work[0, jnp.maximum(total - 1, 0)]
+    work[0, total + 1] = 0
     for extra in range(2):
-        if extra:
-            work[0, total + extra] = 0
         work[1, total + extra] = 0
         work[2, total + extra] = 1
         work[3, total + extra] = 0
-        work[4, total + extra] = -1
+        work[4, total + extra] = none
 
     def prepare(at, s_ref, t_ref):
-        tile = work[0, at]
-        h, r, b = tile // tiles, (tile // per) % rows, tile % per
-        heads_at = pl.ds(pl.multiple_of((first_head + h) * group, group), group)
-        q = q_ref[r, pl.ds(b * blk, blk), heads_at, :].reshape(width, size)
+        q = qbuf[work[0, at]].reshape(width, size)
         scores(q, kbuf[work[1, at]], s_ref, t_ref)
 
     def fix(at, s_ref, t_ref):
         @pl.when(work[2, at] == 1)
         def _():
-            slot = work[1, at] % slots
+            i = work[4, at]
             token = work[3, at] + lax.broadcasted_iota(jnp.int32, (1, width), 1) // group
-            bound = jnp.minimum(token, work[4, at])
-            hide(bound, [work[5 + run, slot] for run in range(runs)], s_ref, t_ref)
+            table = [[work[run_at + 3 * run + j, i] for j in range(3)] for run in range(runs)]
+            hide(token, table, s_ref, t_ref)
 
     def finish(at, s_ref, t_ref):
         absorb(work[0, at], vt_ref[work[1, at]], s_ref, t_ref, m_ref, l_ref, acc_ref)
+
+    for tile in range(heads * tiles):
+        fetch(tile).wait()
 
     @pl.when(total > 0)
     def _():
@@ -267,33 +294,38 @@
         lax.fori_loop(0, heads * tiles, lambda t, _: (write(t).wait(), 0)[1], 0)
 
 
-def step_call(scalars, q_rot, carry, parts, sources, out, last, first_head, blocks, n, group):
+def step_call(scalars, q_rot, carry, parts, chunks, out, last, first_head, blocks, n, group):
     rows, count, _, size = q_rot.shape
-    packed = parts[0].ndim == 4
-    unit_heads, depth, _ = parts[0].shape[-3:]
-    local = depth - rows * count
+    sources = sorted({source for _, units in chunks for source, _ in units})
+    packed = tuple(not isinstance(parts[source], tuple) for source in sources)
+    arrays = []
+    for source in sources:
+        arrays += list(parts[source]) if isinstance(parts[source], tuple) else [parts[source]]
+    unit_heads = arrays[0].shape[-3]
     per = blocks // n
     blk = count // per
     width = blk * group
     tiles = unit_heads * rows * per
-    chunk = 2 * count
-    slots = len(sources) * (local // chunk) + rows
-    items = unit_heads * rows * per * (slots - rows + 1) + 2
+    depth = chunk_units * count
+    items = unit_heads * per * len(chunks)
     fresh, chained = carry is None, last and out is not None
     vmem, anywhere = pl.BlockSpec(memory_space=pltpu.VMEM), pl.BlockSpec(memory_space=pl.ANY)
     state = lambda d: (tiles, d, width)
     f32 = lambda d: jax.ShapeDtypeStruct(state(d), jnp.float32)
     scratch = [
-        pltpu.VMEM((unit_heads * slots, chunk, size), jnp.bfloat16),
-        pltpu.VMEM((unit_heads * slots, size, chunk), jnp.bfloat16),
-        pltpu.VMEM((chunk, width), jnp.float32),
-        pltpu.VMEM((chunk, width), jnp.float32),
+        pltpu.VMEM((unit_heads * len(chunks), depth, size), jnp.bfloat16),
+        pltpu.VMEM((unit_heads * len(chunks), size, depth), jnp.bfloat16),
+        pltpu.VMEM((tiles, blk, group, size), jnp.bfloat16),
+        pltpu.VMEM((depth, width), jnp.float32),
+        pltpu.VMEM((depth, width), jnp.float32),
         pltpu.VMEM((8, width), jnp.float32),
         pltpu.VMEM((8, width), jnp.float32),
-        pltpu.SMEM((5 + chunk // blk, max(items, slots)), jnp.int32),
+        pltpu.SMEM((5 + 3 * depth // blk, items + 2), jnp.int32),
+        pltpu.SemaphoreType.DMA((tiles,)),
     ]
-    operands = [scalars, q_rot] + ([] if fresh else list(carry)) + list(parts)
-    specs = [pl.BlockSpec(memory_space=pltpu.SMEM)] + [vmem] * (len(operands) - 1)
+    q_rot = pltpu.with_memory_space_constraint(q_rot, pltpu.HBM)
+    operands = [scalars, q_rot] + ([] if fresh else list(carry)) + arrays
+    specs = [pl.BlockSpec(memory_space=pltpu.SMEM), pl.BlockSpec(memory_space=pltpu.HBM)] + [vmem] * (len(operands) - 2)
     aliases = {} if fresh or last else {2: 0, 3: 1, 4: 2}
     if last:
         scratch += [
@@ -307,8 +339,8 @@
         shapes, out_specs = jax.ShapeDtypeStruct(q_rot.shape, q_rot.dtype), anywhere
     else:
         shapes, out_specs = [f32(size), f32(8), f32(8)], [vmem] * 3
-    cfg = (n, blocks, blk, first_head, tuple(sources), packed, fresh, last, chained)
-    pairs = items * chunk * width
+    cfg = (n, blocks, blk, first_head, chunks, sources, packed, fresh, last, chained)
+    pairs = items * depth * width
     return pl.pallas_call(
         functools.partial(step_kernel, cfg),
         in_specs=specs,
@@ -316,22 +348,20 @@
         scratch_shapes=scratch,
         out_shape=shapes,
         input_output_aliases=aliases,
-        compiler_params=pltpu.CompilerParams(vmem_limit_bytes=24 * 1024 * 1024),
+        compiler_params=pltpu.CompilerParams(vmem_limit_bytes=(20 if last else 14) * 1024 * 1024),
         cost_estimate=pl.CostEstimate(
             flops=pairs * size * 4, bytes_accessed=1024 * 1024, transcendentals=pairs
         ),
     )(*operands)
 
 
-def turn_kernel(parts, q_ref, cosine_ref, sine_ref, o_ref):
-    i = pl.program_id(0)
-    tokens, _, size = q_ref.shape[1:]
+def turn_kernel(q_ref, cosine_ref, sine_ref, o_ref):
+    size = q_ref.shape[-1]
     x = q_ref[0].astype(jnp.float32)
     cosine = cosine_ref[0][:, None, :]
     sine = sine_ref[0][:, None, :]
     turned = x * cosine + pltpu.roll(x, size // 2, 2) * sine
-    at = pl.ds(pl.multiple_of((i % parts) * tokens, tokens), tokens)
-    o_ref[i // parts, at] = turned.astype(o_ref.dtype)
+    o_ref[0] = turned.astype(o_ref.dtype)
 
 
 def turn_call(queries, cosine, sine):
@@ -339,22 +369,19 @@
     tokens = 16
     parts = count // tokens
     table = pl.BlockSpec((1, tokens, size), lambda i: (i // parts, i % parts, 0))
+    spot = pl.BlockSpec((1, tokens, heads, size), lambda i: (i // parts, i % parts, 0, 0))
     return pl.pallas_call(
-        functools.partial(turn_kernel, parts),
+        turn_kernel,
         grid=(rows * parts,),
-        in_specs=[
-            pl.BlockSpec((1, tokens, heads, size), lambda i: (i // parts, i % parts, 0, 0)),
-            table,
-            table,
-        ],
-        out_specs=pl.BlockSpec(queries.shape, lambda i: (0, 0, 0, 0)),
-        out_shape=jax.ShapeDtypeStruct(queries.shape, queries.dtype),
-        compiler_params=pltpu.CompilerParams(vmem_limit_bytes=16 * 1024 * 1024),
+        in_specs=[spot, table, table],
+        out_specs=spot,
+        out_shape=pltpu.HBM(queries.shape, queries.dtype),
+        compiler_params=pltpu.CompilerParams(vmem_limit_bytes=8 * 1024 * 1024),
         cost_estimate=pl.CostEstimate(
             flops=queries.size * 4, bytes_accessed=queries.size * 4, transcendentals=0
         ),
         name="turn",
-    )(queries, cosine, sine)
+    )(pltpu.with_memory_space_constraint(queries, pltpu.HBM), cosine, sine)
 
 
 def shards(
@@ -425,14 +452,17 @@
     ahead, back, carry = list(own), list(own), [None] * count_u
     out = None
 
-    def step(todo, tied=None, last=False):
-        u, parts, sources = todo
+    parts = [{0: own[u]} for u in range(count_u)]
+    local = prefix_key_rows.shape[1]
+    steps = plan(n, local // count)
+
+    def step(u, s, last=False):
         return step_call(
-            scalars if tied is None else tied,
+            scalars,
             q_rot,
             carry[u],
-            parts,
-            sources,
+            parts[u],
+            steps[s - 1],
             out,
             last,
             firsts[u],
@@ -443,23 +473,17 @@
 
     for u in range(count_u):
         ahead[u], back[u] = send(ahead[u], forward), send(back[u], backward)
-    carry[0] = step((0, [own[0]], [0]))
-    waiting = [(u, [own[u]], [0]) for u in range(1, count_u)]
     for s in range(1, n // 2):
         for u in range(count_u):
-            here, there, tied = lax.optimization_barrier((ahead[u], back[u], scalars))
-            waiting.append((u, [here, there], [s, n - s]))
+            here, there = ahead[u], back[u]
+            parts[u][s], parts[u][n - s] = here, there
             if s + 1 == n // 2:
                 here, there = here[0], there[1]
-            if carry[u] is not None:
-                here, there, carry[u] = lax.optimization_barrier((here, there, carry[u]))
             ahead[u], back[u] = send(here, forward), send(there, backward)
-            todo = waiting.pop(0)
-            carry[todo[0]] = step(todo, tied)
-    for todo in waiting:
-        carry[todo[0]] = step(todo)
+            carry[u] = step(u, s)
     for u in range(count_u):
-        out = step((u, [ahead[u], back[u]], [n // 2]), last=True)
+        parts[u][n // 2] = (ahead[u], back[u])
+        out = step(u, n // 2, last=True)
     return out
 
 

time: 125 us -> 154 us (1.23)
  the two profiles are of different devices: /device:TPU:12 before, /device:TPU:16 now
where the time goes in v1:
time: 154 us; the launch traced here: 153 us
  Pallas kernels  100 us (65%)
  starting transfers between devices  23.6 us (15%)
  waiting for transfers between devices  19.3 us (13%)
  other arithmetic  5.41 us (4%)
  between operations  2.48 us (2%)
  local copies, waits for them, and re-layouts  2.22 us (1%)
    pallas_call x8, Pallas kernels, step_call(): pl.pallas_call(functools.partial(step_kernel, cfg), in_specs=specs, out_s...  89.2 us
    ppermute x16, starting transfers between devices, send(): return lax.ppermute(x, 'ctx', way)  23.6 us
    ppermute x16, waiting for transfers between devices, send(): return lax.ppermute(x, 'ctx', way)  19.3 us
    pallas_call x1, Pallas kernels, turn_call(): pl.pallas_call(turn_kernel, grid=(rows * parts,), in_specs=[spot, table,...  11 us
  transfers between devices with their start and end apart: 16, of which 2 were waited for; matrix products, arithmetic and copies ran while one was open for 1% of the time, Pallas kernels for 57%

profile of v1, /device:TPU:16, one launch (start us, length us, event | category | flops | bytes accessed | tf_op | source)
XLA Modules:
  0.0 153.2 jit_solution(16854222246747819592)
XLA Ops:
  0.0 0.8 dynamic-slice_multiply_fusion
  1.0 1.2 slice_convert_fusion
  2.2 0.7 compare_select_fusion
  3.6 0.8 subtract_convert_fusion
  6.7 1.6 %collective-permute-start.8 = (bf16[2,2,512,128]{3,2,1,0:T(8,128)(2,1)S(1)}, bf16[2,2,512,128]{3,2,1,0:T(8,128)(2,1)S(1)}, u32[]{:S(2)}, u32[]{:S(2)}) collective-permute-start(bf16[2,2,512,128]{3,2,1,0:T(8,128)(2,1)S(1)} %pad_maximum_fusion.1.refs_0_.refs_3_), channel_id=1, source_target_pairs={{0,8},{8,16},{16,24},{24,28},{28,20},{20,12},{12,4},{4,0},{1,9},{9... | collective-permute-start | bytes 1572872 | tf_op jit(solution)/shard_map/ppermute | solution.py:447
  9.0 1.6 %collective-permute-start = (bf16[2,2,512,128]{3,2,1,0:T(8,128)(2,1)S(1)}, bf16[2,2,512,128]{3,2,1,0:T(8,128)(2,1)}, u32[]{:S(2)}, u32[]{:S(2)}) collective-permute-start(bf16[2,2,512,128]{3,2,1,0:T(8,128)(2,1)S(1)} %pad_maximum_fusion.refs_0_.refs_3_), channel_id=1, source_target_pairs={{0,8},{8,16},{16,24},{24,28},{28,20},{20,12},{12,4},{4,0},{1,9},{9... | collective-permute-start | bytes 1572872 | tf_op jit(solution)/shard_map/ppermute | solution.py:447
  11.1 10.5 %collective-permute-done.8.refs_1_.refs_4_ = bf16[2,2,512,128]{3,2,1,0:T(8,128)(2,1)S(1)} collective-permute-done((bf16[2,2,512,128]{3,2,1,0:T(8,128)(2,1)S(1)}, bf16[2,2,512,128]{3,2,1,0:T(8,128)(2,1)S(1)}, u32[]{:S(2)}, u32[]{:S(2)}) %collective-permute-start.8) | collective-permute-done | bytes 524320 | tf_op jit(solution)/shard_map/ppermute | solution.py:447
  21.6 1.6 %collective-permute-start.10 = (bf16[2,2,512,128]{3,2,1,0:T(8,128)(2,1)S(1)}, bf16[2,2,512,128]{3,2,1,0:T(8,128)(2,1)}, u32[]{:S(2)}, u32[]{:S(2)}) collective-permute-start(bf16[2,2,512,128]{3,2,1,0:T(8,128)(2,1)S(1)} %collective-permute-done.8.refs_1_.refs_4_), channel_id=1, source_target_pairs={{0,8},{8,16},{16,24},{24,28},{28,20},{20,12},{12,4},{4,0},{1,9},{9... | collective-permute-start | bytes 1572872 | tf_op jit(solution)/shard_map/ppermute | solution.py:447
  24.2 8.7 %collective-permute-done.refs_1_.refs_4_ = bf16[2,2,512,128]{3,2,1,0:T(8,128)(2,1)} collective-permute-done((bf16[2,2,512,128]{3,2,1,0:T(8,128)(2,1)S(1)}, bf16[2,2,512,128]{3,2,1,0:T(8,128)(2,1)}, u32[]{:S(2)}, u32[]{:S(2)}) %collective-permute-start) | collective-permute-done | bytes 524320 | tf_op jit(solution)/shard_map/ppermute | solution.py:447
  32.9 1.6 %collective-permute-start.2 = (bf16[2,2,512,128]{3,2,1,0:T(8,128)(2,1)}, bf16[2,2,512,128]{3,2,1,0:T(8,128)(2,1)}, u32[]{:S(2)}, u32[]{:S(2)}) collective-permute-start(bf16[2,2,512,128]{3,2,1,0:T(8,128)(2,1)} %collective-permute-done.refs_1_.refs_4_), channel_id=1, source_target_pairs={{0,8},{8,16},{16,24},{24,28},{28,20},{20,12},{12,4},{4,0},{1,9},{9... | collective-permute-start | bytes 1572872 | tf_op jit(solution)/shard_map/ppermute | solution.py:447
  37.1 11.0 %turn.1.q_ref = bf16[2,128,64,128]{3,2,1,0:T(8,128)(2,1)} custom-call(bf16[2,128,64,128]{3,2,1,0:T(8,128)(2,1)} %q_ref.1, f32[2,128,128]{2,1,0:T(8,128)S(1)} %get-tuple-element.66.cosine_ref, f32[2,128,128]{2,1,0:T(8,128)S(1)} %get-tuple-element.67.sine_ref), custom_call_target="tpu_custom_call" | custom-call | flops 8388608 | bytes 8388608 | tf_op jit(solution)/shard_map/turn/pallas_call | solution.py:373
  48.2 7.4 %shard_map.103 = (f32[8,128,1024]{2,1,0:T(8,128)S(1)}, f32[8,8,1024]{2,1,0:T(8,128)S(1)}, f32[8,8,1024]{2,1,0:T(8,128)S(1)}) custom-call(s32[28]{0:T(128)S(1)} %concatenate.29.sc, bf16[2,128,64,128]{3,2,1,0:T(8,128)(2,1)} %turn.1.q_ref, bf16[2,2,512,128]{3,2,1,0:T(8,128)(2,1)S(1)} %pad_maximum_fusion.1.refs_0_.refs_3_, ...), custom_call_target="tpu_custom_call" | custom-call | flops 2147483648 | bytes 1048576 | tf_op jit(solution)/shard_map/pallas_call | solution.py:344
  55.6 1.6 %collective-permute-start.11 = (bf16[2,2,512,128]{3,2,1,0:T(8,128)(2,1)}, bf16[2,2,512,128]{3,2,1,0:T(8,128)(2,1)S(1)}, u32[]{:S(2)}, u32[]{:S(2)}) collective-permute-start(bf16[2,2,512,128]{3,2,1,0:T(8,128)(2,1)} %collective-permute-done.10.refs_5_), channel_id=1, source_target_pairs={{0,8},{8,16},{16,24},{24,28},{28,20},{20,12},{12,4},{4,0},{1,9},{9... | collective-permute-start | bytes 1572872 | tf_op jit(solution)/shard_map/ppermute | solution.py:447
  57.3 8.1 %shard_map.100 = (f32[8,128,1024]{2,1,0:T(8,128)S(1)}, f32[8,8,1024]{2,1,0:T(8,128)S(1)}, f32[8,8,1024]{2,1,0:T(8,128)S(1)}) custom-call(s32[28]{0:T(128)S(1)} %concatenate.29.sc, bf16[2,128,64,128]{3,2,1,0:T(8,128)(2,1)} %turn.1.q_ref, bf16[2,2,512,128]{3,2,1,0:T(8,128)(2,1)S(1)} %pad_maximum_fusion.refs_0_.refs_3_, ...), custom_call_target="tpu_custom_call" | custom-call | flops 2147483648 | bytes 1048576 | tf_op jit(solution)/shard_map/pallas_call | solution.py:344
  65.4 7.3 %collective-permute-start.13 = (bf16[2,2,512,128]{3,2,1,0:T(8,128)(2,1)S(1)}, bf16[2,2,512,128]{3,2,1,0:T(8,128)(2,1)S(1)}, u32[]{:S(2)}, u32[]{:S(2)}) collective-permute-start(bf16[2,2,512,128]{3,2,1,0:T(8,128)(2,1)S(1)} %collective-permute-done.12.refs_5_.refs_7_), channel_id=1, source_target_pairs={{8,0},{16,8},{24,16},{28,24},{20,28},{12,20},{4,12},{0,4},{9,1},{1... | collective-permute-start | bytes 1572872 | tf_op jit(solution)/shard_map/ppermute | solution.py:447
  72.7 2.2 %collective-permute-start.5 = (bf16[2,2,512,128]{3,2,1,0:T(8,128)(2,1)S(1)}, bf16[2,2,512,128]{3,2,1,0:T(8,128)(2,1)S(1)}, u32[]{:S(2)}, u32[]{:S(2)}) collective-permute-start(bf16[2,2,512,128]{3,2,1,0:T(8,128)(2,1)S(1)} %collective-permute-done.4.refs_5_.refs_7_), channel_id=1, source_target_pairs={{8,0},{16,8},{24,16},{28,24},{20,28},{12,20},{4,12},{0,4},{9,1},{1... | collective-permute-start | bytes 1572872 | tf_op jit(solution)/shard_map/ppermute | solution.py:447
  74.9 11.8 %shard_map.104 = (f32[8,128,1024]{2,1,0:T(8,128)S(1)}, f32[8,8,1024]{2,1,0:T(8,128)S(1)}, f32[8,8,1024]{2,1,0:T(8,128)S(1)}) custom-call(s32[28]{0:T(128)S(1)} %concatenate.29.sc, bf16[2,128,64,128]{3,2,1,0:T(8,128)(2,1)} %turn.1.q_ref, f32[8,128,1024]{2,1,0:T(8,128)S(1)} %get-tuple-element.32.refs_0_, ...), custom_call_target="tpu_custom_call", output_to_operand_aliasing={{0}: (2, {}), {1}: (3, {}), {2}: (4, {})} | custom-call | flops 2147483648 | bytes 1048576 | tf_op jit(solution)/shard_map/pallas_call | solution.py:344
  86.7 12.1 %shard_map.101 = (f32[8,128,1024]{2,1,0:T(8,128)S(1)}, f32[8,8,1024]{2,1,0:T(8,128)S(1)}, f32[8,8,1024]{2,1,0:T(8,128)S(1)}) custom-call(s32[28]{0:T(128)S(1)} %concatenate.29.sc, bf16[2,128,64,128]{3,2,1,0:T(8,128)(2,1)} %turn.1.q_ref, f32[8,128,1024]{2,1,0:T(8,128)S(1)} %get-tuple-element.23.refs_0_, ...), custom_call_target="tpu_custom_call", output_to_operand_aliasing={{0}: (2, {}), {1}: (3, {}), {2}: (4, {})} | custom-call | flops 2147483648 | bytes 1048576 | tf_op jit(solution)/shard_map/pallas_call | solution.py:344
  99.0 2.1 %collective-permute-start.15 = (bf16[2,512,128]{2,1,0:T(8,128)(2,1)S(1)}, bf16[2,512,128]{2,1,0:T(8,128)(2,1)S(1)}, u32[]{:S(2)}, u32[]{:S(2)}) collective-permute-start(bf16[2,512,128]{2,1,0:T(8,128)(2,1)S(1)} %slice_bitcast_fusion), channel_id=1, source_target_pairs={{8,0},{16,8},{24,16},{28,24},{20,28},{12,20},{4,12},{0,4},{9,1},{1... | collective-permute-start | bytes 786440 | tf_op jit(solution)/shard_map/ppermute | solution.py:447
  101.2 2.1 %collective-permute-start.7 = (bf16[2,512,128]{2,1,0:T(8,128)(2,1)S(1)}, bf16[2,512,128]{2,1,0:T(8,128)(2,1)S(1)}, u32[]{:S(2)}, u32[]{:S(2)}) collective-permute-start(bf16[2,512,128]{2,1,0:T(8,128)(2,1)S(1)} %slice_bitcast_fusion.2), channel_id=1, source_target_pairs={{8,0},{16,8},{24,16},{28,24},{20,28},{12,20},{4,12},{0,4},{9,1},{1... | collective-permute-start | bytes 786440 | tf_op jit(solution)/shard_map/ppermute | solution.py:447
  103.2 11.3 %shard_map.105 = (f32[8,128,1024]{2,1,0:T(8,128)S(1)}, f32[8,8,1024]{2,1,0:T(8,128)S(1)}, f32[8,8,1024]{2,1,0:T(8,128)S(1)}) custom-call(s32[28]{0:T(128)S(1)} %concatenate.29.sc, bf16[2,128,64,128]{3,2,1,0:T(8,128)(2,1)} %turn.1.q_ref, f32[8,128,1024]{2,1,0:T(8,128)S(1)} %get-tuple-element.35.refs_0_, ...), custom_call_target="tpu_custom_call", output_to_operand_aliasing={{0}: (2, {}), {1}: (3, {}), {2}: (4, {})} | custom-call | flops 2147483648 | bytes 1048576 | tf_op jit(solution)/shard_map/pallas_call | solution.py:344
  114.5 11.6 %shard_map.102 = (f32[8,128,1024]{2,1,0:T(8,128)S(1)}, f32[8,8,1024]{2,1,0:T(8,128)S(1)}, f32[8,8,1024]{2,1,0:T(8,128)S(1)}) custom-call(s32[28]{0:T(128)S(1)} %concatenate.29.sc, bf16[2,128,64,128]{3,2,1,0:T(8,128)(2,1)} %turn.1.q_ref, f32[8,128,1024]{2,1,0:T(8,128)S(1)} %get-tuple-element.26.refs_0_, ...), custom_call_target="tpu_custom_call", output_to_operand_aliasing={{0}: (2, {}), {1}: (3, {}), {2}: (4, {})} | custom-call | flops 2147483648 | bytes 1048576 | tf_op jit(solution)/shard_map/pallas_call | solution.py:344
  126.1 13.4 %shard_map.106.refs_8_ = bf16[2,128,64,128]{3,2,1,0:T(8,128)(2,1)} custom-call(s32[28]{0:T(128)S(1)} %concatenate.29.sc, bf16[2,128,64,128]{3,2,1,0:T(8,128)(2,1)} %turn.1.q_ref, f32[8,128,1024]{2,1,0:T(8,128)S(1)} %get-tuple-element.38.refs_0_, f32[8,8,1024]{2,1,0:T(8,128)S(1)} %get-tuple-element.39.refs_1_, f32[8,8,1024]{2,1,0:T(8,128)S(1)} %get-tuple-element.40.refs_2_, ...), custom_call_target="tpu_custom_call" | custom-call | flops 2147483648 | bytes 1048576 | tf_op jit(solution)/shard_map/pallas_call | solution.py:344
  139.6 13.4 %shard_map.107 = bf16[2,128,64,128]{3,2,1,0:T(8,128)(2,1)} custom-call(s32[28]{0:T(128)S(1)} %concatenate.29.sc, bf16[2,128,64,128]{3,2,1,0:T(8,128)(2,1)} %turn.1.q_ref, f32[8,128,1024]{2,1,0:T(8,128)S(1)} %get-tuple-element.29.refs_0_, f32[8,8,1024]{2,1,0:T(8,128)S(1)} %get-tuple-element.30.refs_1_, ...), custom_call_target="tpu_custom_call", output_to_operand_aliasing={{}: (10, {})} | custom-call | flops 2147483648 | bytes 1048576 | tf_op jit(solution)/shard_map/pallas_call | solution.py:344
  (63 shorter events, 6.1 us)
Async XLA Ops:
  0.0 5.8 %copy-start = (bf16[2,256,4,128]{3,2,1,0:T(4,128)(2,1)S(1)}, bf16[2,256,4,128]{3,2,1,0:T(4,128)(2,1)}, u32[]{:S(2)}) copy-start(bf16[2,256,4,128]{3,2,1,0:T(4,128)(2,1)} %param.13) | copy-start | bytes 1572868
  0.0 6.0 %copy-start.1 = (bf16[2,256,4,128]{3,2,1,0:T(4,128)(2,1)S(1)}, bf16[2,256,4,128]{3,2,1,0:T(4,128)(2,1)}, u32[]{:S(2)}) copy-start(bf16[2,256,4,128]{3,2,1,0:T(4,128)(2,1)} %param.14) | copy-start | bytes 1572868
  2.2 4.2 %copy-start.2 = (bf16[2,128,4,128]{3,2,1,0:T(4,128)(2,1)S(1)}, bf16[2,128,4,128]{3,2,1,0:T(4,128)(2,1)}, u32[]{:S(2)}) copy-start(bf16[2,128,4,128]{3,2,1,0:T(4,128)(2,1)} %param.12) | copy-start | bytes 786436
  6.2 17.0 %copy-start.3 = (s32[2]{0:T(128)S(1)}, s32[2]{0:T(128)}, u32[]{:S(2)}) copy-start(s32[2]{0:T(128)} %param.15) | copy-start | bytes 28
  6.2 30.7 %copy-start.4 = (s32[2]{0:T(128)S(1)}, s32[2]{0:T(128)}, u32[]{:S(2)}) copy-start(s32[2]{0:T(128)} %param.16) | copy-start | bytes 28
  6.2 30.7 %copy-start.5 = (s32[16]{0:T(128)S(1)}, s32[16]{0:T(128)}, u32[]{:S(2)}) copy-start(s32[16]{0:T(128)} %param.18) | copy-start | bytes 196
  6.7 14.8 %collective-permute-start.8 = (bf16[2,2,512,128]{3,2,1,0:T(8,128)(2,1)S(1)}, bf16[2,2,512,128]{3,2,1,0:T(8,128)(2,1)S(1)}, u32[]{:S(2)}, u32[]{:S(2)}) collective-permute-start(bf16[2,2,512,128]{3,2,1,0:T(8,128)(2,1)S(1)} %pad_maximum_fusion.1.refs_0_.refs_3_), channel_id=1, source_target_pairs={{0,8},{8,16},{16,24},{24,28},{28,20},{20,12},{12,4},{4,0},{1,9},{9... | collective-permute-start | bytes 1572872 | tf_op jit(solution)/shard_map/ppermute | solution.py:447
  8.4 15.4 %collective-permute-start.9 = (bf16[2,2,512,128]{3,2,1,0:T(8,128)(2,1)S(1)}, bf16[2,2,512,128]{3,2,1,0:T(8,128)(2,1)S(1)}, u32[]{:S(2)}, u32[]{:S(2)}) collective-permute-start(bf16[2,2,512,128]{3,2,1,0:T(8,128)(2,1)S(1)} %pad_maximum_fusion.1.refs_0_.refs_3_), channel_id=1, source_target_pairs={{8,0},{16,8},{24,16},{28,24},{20,28},{12,20},{4,12},{0,4},{9,1},{1... | collective-permute-start | bytes 1572872 | tf_op jit(solution)/shard_map/ppermute | solution.py:447
  9.0 23.9 %collective-permute-start = (bf16[2,2,512,128]{3,2,1,0:T(8,128)(2,1)S(1)}, bf16[2,2,512,128]{3,2,1,0:T(8,128)(2,1)}, u32[]{:S(2)}, u32[]{:S(2)}) collective-permute-start(bf16[2,2,512,128]{3,2,1,0:T(8,128)(2,1)S(1)} %pad_maximum_fusion.refs_0_.refs_3_), channel_id=1, source_target_pairs={{0,8},{8,16},{16,24},{24,28},{28,20},{20,12},{12,4},{4,0},{1,9},{9... | collective-permute-start | bytes 1572872 | tf_op jit(solution)/shard_map/ppermute | solution.py:447
  10.6 23.9 %collective-permute-start.1 = (bf16[2,2,512,128]{3,2,1,0:T(8,128)(2,1)S(1)}, bf16[2,2,512,128]{3,2,1,0:T(8,128)(2,1)}, u32[]{:S(2)}, u32[]{:S(2)}) collective-permute-start(bf16[2,2,512,128]{3,2,1,0:T(8,128)(2,1)S(1)} %pad_maximum_fusion.refs_0_.refs_3_), channel_id=1, source_target_pairs={{8,0},{16,8},{24,16},{28,24},{20,28},{12,20},{4,12},{0,4},{9,1},{1... | collective-permute-start | bytes 1572872 | tf_op jit(solution)/shard_map/ppermute | solution.py:447
  21.6 34.0 %collective-permute-start.10 = (bf16[2,2,512,128]{3,2,1,0:T(8,128)(2,1)S(1)}, bf16[2,2,512,128]{3,2,1,0:T(8,128)(2,1)}, u32[]{:S(2)}, u32[]{:S(2)}) collective-permute-start(bf16[2,2,512,128]{3,2,1,0:T(8,128)(2,1)S(1)} %collective-permute-done.8.refs_1_.refs_4_), channel_id=1, source_target_pairs={{0,8},{8,16},{16,24},{24,28},{28,20},{20,12},{12,4},{4,0},{1,9},{9... | collective-permute-start | bytes 1572872 | tf_op jit(solution)/shard_map/ppermute | solution.py:447
  23.8 41.6 %collective-permute-start.12 = (bf16[2,2,512,128]{3,2,1,0:T(8,128)(2,1)S(1)}, bf16[2,2,512,128]{3,2,1,0:T(8,128)(2,1)S(1)}, u32[]{:S(2)}, u32[]{:S(2)}) collective-permute-start(bf16[2,2,512,128]{3,2,1,0:T(8,128)(2,1)S(1)} %collective-permute-done.9.refs_2_.refs_6_), channel_id=1, source_target_pairs={{8,0},{16,8},{24,16},{28,24},{20,28},{12,20},{4,12},{0,4},{9,1},{1... | collective-permute-start | bytes 1572872 | tf_op jit(solution)/shard_map/ppermute | solution.py:447
  32.9 39.7 %collective-permute-start.2 = (bf16[2,2,512,128]{3,2,1,0:T(8,128)(2,1)}, bf16[2,2,512,128]{3,2,1,0:T(8,128)(2,1)}, u32[]{:S(2)}, u32[]{:S(2)}) collective-permute-start(bf16[2,2,512,128]{3,2,1,0:T(8,128)(2,1)} %collective-permute-done.refs_1_.refs_4_), channel_id=1, source_target_pairs={{0,8},{8,16},{16,24},{24,28},{28,20},{20,12},{12,4},{4,0},{1,9},{9... | collective-permute-start | bytes 1572872 | tf_op jit(solution)/shard_map/ppermute | solution.py:447
  34.5 38.1 %collective-permute-start.4 = (bf16[2,2,512,128]{3,2,1,0:T(8,128)(2,1)}, bf16[2,2,512,128]{3,2,1,0:T(8,128)(2,1)S(1)}, u32[]{:S(2)}, u32[]{:S(2)}) collective-permute-start(bf16[2,2,512,128]{3,2,1,0:T(8,128)(2,1)} %collective-permute-done.1.refs_2_.refs_6_), channel_id=1, source_target_pairs={{8,0},{16,8},{24,16},{28,24},{20,28},{12,20},{4,12},{0,4},{9,1},{1... | collective-permute-start | bytes 1572872 | tf_op jit(solution)/shard_map/ppermute | solution.py:447
  55.6 43.2 %collective-permute-start.11 = (bf16[2,2,512,128]{3,2,1,0:T(8,128)(2,1)}, bf16[2,2,512,128]{3,2,1,0:T(8,128)(2,1)S(1)}, u32[]{:S(2)}, u32[]{:S(2)}) collective-permute-start(bf16[2,2,512,128]{3,2,1,0:T(8,128)(2,1)} %collective-permute-done.10.refs_5_), channel_id=1, source_target_pairs={{0,8},{8,16},{16,24},{24,28},{28,20},{20,12},{12,4},{4,0},{1,9},{9... | collective-permute-start | bytes 1572872 | tf_op jit(solution)/shard_map/ppermute | solution.py:447
  65.4 33.5 %collective-permute-start.13 = (bf16[2,2,512,128]{3,2,1,0:T(8,128)(2,1)S(1)}, bf16[2,2,512,128]{3,2,1,0:T(8,128)(2,1)S(1)}, u32[]{:S(2)}, u32[]{:S(2)}) collective-permute-start(bf16[2,2,512,128]{3,2,1,0:T(8,128)(2,1)S(1)} %collective-permute-done.12.refs_5_.refs_7_), channel_id=1, source_target_pairs={{8,0},{16,8},{24,16},{28,24},{20,28},{12,20},{4,12},{0,4},{9,1},{1... | collective-permute-start | bytes 1572872 | tf_op jit(solution)/shard_map/ppermute | solution.py:447
  72.6 28.4 %collective-permute-start.3 = (bf16[2,2,512,128]{3,2,1,0:T(8,128)(2,1)}, bf16[2,2,512,128]{3,2,1,0:T(8,128)(2,1)S(1)}, u32[]{:S(2)}, u32[]{:S(2)}) collective-permute-start(bf16[2,2,512,128]{3,2,1,0:T(8,128)(2,1)} %collective-permute-done.2.refs_5_), channel_id=1, source_target_pairs={{0,8},{8,16},{16,24},{24,28},{28,20},{20,12},{12,4},{4,0},{1,9},{9... | collective-permute-start | bytes 1572872 | tf_op jit(solution)/shard_map/ppermute | solution.py:447
  72.7 28.5 %collective-permute-start.5 = (bf16[2,2,512,128]{3,2,1,0:T(8,128)(2,1)S(1)}, bf16[2,2,512,128]{3,2,1,0:T(8,128)(2,1)S(1)}, u32[]{:S(2)}, u32[]{:S(2)}) collective-permute-start(bf16[2,2,512,128]{3,2,1,0:T(8,128)(2,1)S(1)} %collective-permute-done.4.refs_5_.refs_7_), channel_id=1, source_target_pairs={{8,0},{16,8},{24,16},{28,24},{20,28},{12,20},{4,12},{0,4},{9,1},{1... | collective-permute-start | bytes 1572872 | tf_op jit(solution)/shard_map/ppermute | solution.py:447
  98.9 27.2 %collective-permute-start.14 = (bf16[2,512,128]{2,1,0:T(8,128)(2,1)S(1)}, bf16[2,512,128]{2,1,0:T(8,128)(2,1)S(1)}, u32[]{:S(2)}, u32[]{:S(2)}) collective-permute-start(bf16[2,512,128]{2,1,0:T(8,128)(2,1)S(1)} %slice_bitcast_fusion.1), channel_id=1, source_target_pairs={{0,8},{8,16},{16,24},{24,28},{28,20},{20,12},{12,4},{4,0},{1,9},{9... | collective-permute-start | bytes 786440 | tf_op jit(solution)/shard_map/ppermute | solution.py:447
  99.0 27.1 %collective-permute-start.15 = (bf16[2,512,128]{2,1,0:T(8,128)(2,1)S(1)}, bf16[2,512,128]{2,1,0:T(8,128)(2,1)S(1)}, u32[]{:S(2)}, u32[]{:S(2)}) collective-permute-start(bf16[2,512,128]{2,1,0:T(8,128)(2,1)S(1)} %slice_bitcast_fusion), channel_id=1, source_target_pairs={{8,0},{16,8},{24,16},{28,24},{20,28},{12,20},{4,12},{0,4},{9,1},{1... | collective-permute-start | bytes 786440 | tf_op jit(solution)/shard_map/ppermute | solution.py:447
  101.0 38.5 %collective-permute-start.6 = (bf16[2,512,128]{2,1,0:T(8,128)(2,1)S(1)}, bf16[2,512,128]{2,1,0:T(8,128)(2,1)S(1)}, u32[]{:S(2)}, u32[]{:S(2)}) collective-permute-start(bf16[2,512,128]{2,1,0:T(8,128)(2,1)S(1)} %slice_bitcast_fusion.3), channel_id=1, source_target_pairs={{0,8},{8,16},{16,24},{24,28},{28,20},{20,12},{12,4},{4,0},{1,9},{9... | collective-permute-start | bytes 786440 | tf_op jit(solution)/shard_map/ppermute | solution.py:447
  101.2 38.4 %collective-permute-start.7 = (bf16[2,512,128]{2,1,0:T(8,128)(2,1)S(1)}, bf16[2,512,128]{2,1,0:T(8,128)(2,1)S(1)}, u32[]{:S(2)}, u32[]{:S(2)}) collective-permute-start(bf16[2,512,128]{2,1,0:T(8,128)(2,1)S(1)} %slice_bitcast_fusion.2), channel_id=1, source_target_pairs={{8,0},{16,8},{24,16},{28,24},{20,28},{12,20},{4,12},{0,4},{9,1},{1... | collective-permute-start | bytes 786440 | tf_op jit(solution)/shard_map/ppermute | solution.py:447

commit v2 on v1

--- a/solution.py
+++ b/solution.py
@@ -12,7 +12,7 @@
 neg_large = -1e30
 log2e = 1.4426950408889634
 streams = 2
-chunk_units = 4
+chunk_units = 2
 far = 1 << 29
 
 
@@ -94,14 +94,14 @@
 
 def plan(n, cache_units):
     half = n // 2
-    steps, partial, prefill = [], [], []
-    for s in range(1, half + 1):
-        arrived = [s, n - s] if s < half else [half]
-        for source in ([0] if s == 1 else []) + arrived:
-            partial += [(source, c) for c in range(cache_units)] + [(source, None)]
+    steps, cache, partial, prefill = [], [], [], []
+    for s in range(half + 1):
+        for source in [s] if s in (0, half) else [s, n - s]:
+            cache += [(source, c) for c in range(cache_units)]
+            partial += [(source, None)]
             prefill += [(source, None)]
         chunks = []
-        for kind, queue in ((0, partial), (1, prefill)):
+        for kind, queue in ((0, cache), (0, partial), (1, prefill)):
             while len(queue) >= chunk_units or (s == half and queue):
                 chunks.append((kind, tuple(queue[:chunk_units])))
                 del queue[:chunk_units]
@@ -129,7 +129,7 @@
         stage, o_sem = refs[-5:-3]
     else:
         acc_ref, m_ref, l_ref = take(3)
-    kbuf, vt_ref, qbuf, s0, s1, t0, t1, work, q_sem = take(9)
+    kbuf, vt_ref, s0, s1, t0, t1, work = take(7)
     rows, count, _, size = q_ref.shape
     heads = pairs[sources[0]][0].shape[0]
     width = acc_ref.shape[2]
@@ -142,16 +142,7 @@
     row_of = lambda kind: sc[0] if kind == 0 else 1 - sc[0]
     run_at = 5
 
-    def fetch(tile):
-        h, r, b = tile // tiles, (tile // per) % rows, tile % per
-        heads_at = pl.ds((first_head + h) * group, group)
-        return pltpu.make_async_copy(
-            q_ref.at[r, pl.ds(b * blk, blk), heads_at], qbuf.at[tile], q_sem.at[tile]
-        )
-
-    for tile in range(heads * tiles):
-        fetch(tile).start()
-
+    cached, fresh_runs = [], []
     for i, (kind, units) in enumerate(chunks):
         row = row_of(kind)
         live = sc[2 + row]
@@ -170,12 +161,20 @@
                 values.append(jnp.zeros((rest, size), keys[0].dtype))
             kbuf[h * len(chunks) + i] = jnp.concatenate(keys, 0)
             vt_ref[h * len(chunks) + i] = jnp.concatenate(values, 0).T
+        hit, cut, new = jnp.int32(0), jnp.int32(int(len(units) < chunk_units)), []
         for source, c in units:
-            for b in range(per):
-                if c is None:
-                    table.append((sc[order + sc[4 + source] * per + b] * blk, 0, live - 1))
-                else:
-                    table.append((sc[4 + source] * local + c * count + b * blk, far, sc[1] - 1))
+            if c is None:
+                for b in range(per):
+                    base = sc[order + sc[4 + source] * per + b] * blk
+                    table.append((base, 0, live - 1))
+                    new.append(base)
+            else:
+                base = sc[4 + source] * local + c * count
+                table += [(base + b * blk, far, sc[1] - 1) for b in range(per)]
+                hit = hit | (base < sc[1]).astype(jnp.int32)
+                cut = cut | (base + count > sc[1]).astype(jnp.int32)
+        cached.append((hit, cut))
+        fresh_runs.append(new)
         table += [(0, 0, -1)] * (runs - len(table))
         for run, entry in enumerate(table):
             for j, value in enumerate(entry):
@@ -196,17 +195,12 @@
         for b in range(per):
             first = sc[order + sc[4] * per + b] * blk
 
-            def look(run, state, first=first, i=i):
-                seen, hidden = state
-                base, offset, limit = (work[run_at + 3 * run + j, i] for j in range(3))
-                least = jnp.minimum(first + offset, limit)
-                most = jnp.minimum(first + blk - 1 + offset, limit)
-                seen = seen | (base <= most).astype(jnp.int32)
-                return seen, hidden | (base + blk - 1 > least).astype(jnp.int32)
-
-            state = (jnp.int32(0), jnp.int32(0))
-            for run in range(runs):
-                state = look(run, state)
+            state = list(cached[i])
+            least = jnp.minimum(first, sc[2 + row] - 1)
+            most = jnp.minimum(first + blk, sc[2 + row]) - 1
+            for base in fresh_runs[i]:
+                state[0] = state[0] | (base <= most).astype(jnp.int32)
+                state[1] = state[1] | (base + blk - 1 > least).astype(jnp.int32)
             go = jnp.where(first < sc[2 + row], state[0], 0)
             for h in range(heads):
                 work[0, total] = (h * rows + row) * per + b
@@ -228,7 +222,10 @@
         work[4, total + extra] = none
 
     def prepare(at, s_ref, t_ref):
-        q = qbuf[work[0, at]].reshape(width, size)
+        tile = work[0, at]
+        h, r, b = tile // tiles, (tile // per) % rows, tile % per
+        heads_at = pl.ds(pl.multiple_of((first_head + h) * group, group), group)
+        q = q_ref[r, pl.ds(b * blk, blk), heads_at, :].reshape(width, size)
         scores(q, kbuf[work[1, at]], s_ref, t_ref)
 
     def fix(at, s_ref, t_ref):
@@ -241,9 +238,6 @@
 
     def finish(at, s_ref, t_ref):
         absorb(work[0, at], vt_ref[work[1, at]], s_ref, t_ref, m_ref, l_ref, acc_ref)
-
-    for tile in range(heads * tiles):
-        fetch(tile).wait()
 
     @pl.when(total > 0)
     def _():
@@ -315,17 +309,14 @@
     scratch = [
         pltpu.VMEM((unit_heads * len(chunks), depth, size), jnp.bfloat16),
         pltpu.VMEM((unit_heads * len(chunks), size, depth), jnp.bfloat16),
-        pltpu.VMEM((tiles, blk, group, size), jnp.bfloat16),
         pltpu.VMEM((depth, width), jnp.float32),
         pltpu.VMEM((depth, width), jnp.float32),
         pltpu.VMEM((8, width), jnp.float32),
         pltpu.VMEM((8, width), jnp.float32),
         pltpu.SMEM((5 + 3 * depth // blk, items + 2), jnp.int32),
-        pltpu.SemaphoreType.DMA((tiles,)),
     ]
-    q_rot = pltpu.with_memory_space_constraint(q_rot, pltpu.HBM)
     operands = [scalars, q_rot] + ([] if fresh else list(carry)) + arrays
-    specs = [pl.BlockSpec(memory_space=pltpu.SMEM), pl.BlockSpec(memory_space=pltpu.HBM)] + [vmem] * (len(operands) - 2)
+    specs = [pl.BlockSpec(memory_space=pltpu.SMEM)] + [vmem] * (len(operands) - 1)
     aliases = {} if fresh or last else {2: 0, 3: 1, 4: 2}
     if last:
         scratch += [
@@ -348,35 +339,40 @@
         scratch_shapes=scratch,
         out_shape=shapes,
         input_output_aliases=aliases,
-        compiler_params=pltpu.CompilerParams(vmem_limit_bytes=(20 if last else 14) * 1024 * 1024),
+        compiler_params=pltpu.CompilerParams(vmem_limit_bytes=24 * 1024 * 1024),
         cost_estimate=pl.CostEstimate(
             flops=pairs * size * 4, bytes_accessed=1024 * 1024, transcendentals=pairs
         ),
     )(*operands)
 
 
-def turn_kernel(q_ref, cosine_ref, sine_ref, o_ref):
-    size = q_ref.shape[-1]
+def turn_kernel(parts, q_ref, cosine_ref, sine_ref, o_ref):
+    i = pl.program_id(0)
+    tokens, _, size = q_ref.shape[1:]
     x = q_ref[0].astype(jnp.float32)
     cosine = cosine_ref[0][:, None, :]
     sine = sine_ref[0][:, None, :]
     turned = x * cosine + pltpu.roll(x, size // 2, 2) * sine
-    o_ref[0] = turned.astype(o_ref.dtype)
+    at = pl.ds(pl.multiple_of((i % parts) * tokens, tokens), tokens)
+    o_ref[i // parts, at] = turned.astype(o_ref.dtype)
 
 
 def turn_call(queries, cosine, sine):
     rows, count, heads, size = queries.shape
-    tokens = 16
+    tokens = count // 2
     parts = count // tokens
     table = pl.BlockSpec((1, tokens, size), lambda i: (i // parts, i % parts, 0))
-    spot = pl.BlockSpec((1, tokens, heads, size), lambda i: (i // parts, i % parts, 0, 0))
     return pl.pallas_call(
-        turn_kernel,
+        functools.partial(turn_kernel, parts),
         grid=(rows * parts,),
-        in_specs=[spot, table, table],
-        out_specs=spot,
-        out_shape=pltpu.HBM(queries.shape, queries.dtype),
-        compiler_params=pltpu.CompilerParams(vmem_limit_bytes=8 * 1024 * 1024),
+        in_specs=[
+            pl.BlockSpec((1, tokens, heads, size), lambda i: (i // parts, i % parts, 0, 0)),
+            table,
+            table,
+        ],
+        out_specs=pl.BlockSpec(queries.shape, lambda i: (0, 0, 0, 0)),
+        out_shape=jax.ShapeDtypeStruct(queries.shape, queries.dtype),
+        compiler_params=pltpu.CompilerParams(vmem_limit_bytes=10 * 1024 * 1024),
         cost_estimate=pl.CostEstimate(
             flops=queries.size * 4, bytes_accessed=queries.size * 4, transcendentals=0
         ),
@@ -462,7 +458,7 @@
             q_rot,
             carry[u],
             parts[u],
-            steps[s - 1],
+            steps[s],
             out,
             last,
             firsts[u],
@@ -473,6 +469,8 @@
 
     for u in range(count_u):
         ahead[u], back[u] = send(ahead[u], forward), send(back[u], backward)
+    for u in range(count_u):
+        carry[u] = step(u, 0)
     for s in range(1, n // 2):
         for u in range(count_u):
             here, there = ahead[u], back[u]

time: 154 us -> 122 us (0.79)
  the two profiles are of different devices: /device:TPU:16 before, /device:TPU:18 now
where the time goes in v2:
time: 122 us; the launch traced here: 121 us
  Pallas kernels  68.6 us (56%)
  waiting for transfers between devices  22.5 us (18%)
  starting transfers between devices  19.9 us (16%)
  other arithmetic  5.42 us (4%)
  between operations  2.55 us (2%)
  local copies, waits for them, and re-layouts  2.3 us (2%)
    pallas_call x10, Pallas kernels, step_call(): pl.pallas_call(functools.partial(step_kernel, cfg), in_specs=specs, out_s...  64.4 us
    ppermute x16, waiting for transfers between devices, send(): return lax.ppermute(x, 'ctx', way)  22.5 us
    ppermute x16, starting transfers between devices, send(): return lax.ppermute(x, 'ctx', way)  19.9 us
    pallas_call x1, Pallas kernels, turn_call(): pl.pallas_call(functools.partial(turn_kernel, parts), grid=(rows * parts,...  4.13 us
  transfers between devices with their start and end apart: 16, of which 3 were waited for; matrix products, arithmetic and copies ran while one was open for 1% of the time, Pallas kernels for 50%

profile of v2, /device:TPU:18, one launch (start us, length us, event | category | flops | bytes accessed | tf_op | source)
XLA Modules:
  0.0 121.3 jit_solution(5550164856271276192)
XLA Ops:
  0.0 0.8 dynamic-slice_multiply_fusion
  1.0 1.2 %slice_convert_fusion = (f32[2,128,2,128]{3,2,1,0:T(2,128)S(1)}, f32[2,128,2,128]{3,2,1,0:T(2,128)S(1)}) fusion(bf16[2,128,4,128]{3,2,1,0:T(4,128)(2,1)} %param.11), kind=kLoop, calls=%fused_computation.29 | loop fusion | flops 131072 | bytes 786432 | tf_op jit(solution)/shard_map/convert_element_type | solution.py:45
  3.6 0.8 subtract_convert_fusion
  7.3 1.6 %collective-permute-start.9 = (bf16[2,2,512,128]{3,2,1,0:T(8,128)(2,1)S(1)}, bf16[2,2,512,128]{3,2,1,0:T(8,128)(2,1)S(1)}, u32[]{:S(2)}, u32[]{:S(2)}) collective-permute-start(bf16[2,2,512,128]{3,2,1,0:T(8,128)(2,1)S(1)} %pad_maximum_fusion.1.refs_0_.refs_3_), channel_id=1, source_target_pairs={{8,0},{16,8},{24,16},{28,24},{20,28},{12,20},{4,12},{0,4},{9,1},{1... | collective-permute-start | bytes 1572872 | tf_op jit(solution)/shard_map/ppermute | solution.py:443
  9.5 1.6 %collective-permute-start.1 = (bf16[2,2,512,128]{3,2,1,0:T(8,128)(2,1)S(1)}, bf16[2,2,512,128]{3,2,1,0:T(8,128)(2,1)S(1)}, u32[]{:S(2)}, u32[]{:S(2)}) collective-permute-start(bf16[2,2,512,128]{3,2,1,0:T(8,128)(2,1)S(1)} %pad_maximum_fusion.refs_0_.refs_3_), channel_id=1, source_target_pairs={{8,0},{16,8},{24,16},{28,24},{20,28},{12,20},{4,12},{0,4},{9,1},{1... | collective-permute-start | bytes 1572872 | tf_op jit(solution)/shard_map/ppermute | solution.py:443
  11.2 10.5 %collective-permute-done.8.refs_4_ = bf16[2,2,512,128]{3,2,1,0:T(8,128)(2,1)} collective-permute-done((bf16[2,2,512,128]{3,2,1,0:T(8,128)(2,1)S(1)}, bf16[2,2,512,128]{3,2,1,0:T(8,128)(2,1)}, u32[]{:S(2)}, u32[]{:S(2)}) %collective-permute-start.8) | collective-permute-done | bytes 524320 | tf_op jit(solution)/shard_map/ppermute | solution.py:443
  22.8 1.6 %collective-permute-start.11 = (bf16[2,2,512,128]{3,2,1,0:T(8,128)(2,1)S(1)}, bf16[2,2,512,128]{3,2,1,0:T(8,128)(2,1)S(1)}, u32[]{:S(2)}, u32[]{:S(2)}) collective-permute-start(bf16[2,2,512,128]{3,2,1,0:T(8,128)(2,1)S(1)} %collective-permute-done.9.refs_5_), channel_id=1, source_target_pairs={{8,0},{16,8},{24,16},{28,24},{20,28},{12,20},{4,12},{0,4},{9,1},{1... | collective-permute-start | bytes 1572872 | tf_op jit(solution)/shard_map/ppermute | solution.py:443
  24.4 8.5 %collective-permute-done.refs_4_ = bf16[2,2,512,128]{3,2,1,0:T(8,128)(2,1)} collective-permute-done((bf16[2,2,512,128]{3,2,1,0:T(8,128)(2,1)S(1)}, bf16[2,2,512,128]{3,2,1,0:T(8,128)(2,1)}, u32[]{:S(2)}, u32[]{:S(2)}) %collective-permute-start) | collective-permute-done | bytes 524320 | tf_op jit(solution)/shard_map/ppermute | solution.py:443
  33.4 1.6 %collective-permute-start.3 = (bf16[2,2,512,128]{3,2,1,0:T(8,128)(2,1)S(1)}, bf16[2,2,512,128]{3,2,1,0:T(8,128)(2,1)S(1)}, u32[]{:S(2)}, u32[]{:S(2)}) collective-permute-start(bf16[2,2,512,128]{3,2,1,0:T(8,128)(2,1)S(1)} %collective-permute-done.1.refs_5_), channel_id=1, source_target_pairs={{8,0},{16,8},{24,16},{28,24},{20,28},{12,20},{4,12},{0,4},{9,1},{1... | collective-permute-start | bytes 1572872 | tf_op jit(solution)/shard_map/ppermute | solution.py:443
  37.0 4.1 %turn.1.q_ref = bf16[2,128,64,128]{3,2,1,0:T(8,128)(2,1)S(1)} custom-call(bf16[2,128,64,128]{3,2,1,0:T(8,128)(2,1)} %q_ref.1, f32[2,128,128]{2,1,0:T(8,128)S(1)} %get-tuple-element.78.cosine_ref, f32[2,128,128]{2,1,0:T(8,128)S(1)} %get-tuple-element.79.sine_ref), custom_call_target="tpu_custom_call" | custom-call | flops 8388608 | bytes 8388608 | tf_op jit(solution)/shard_map/turn/pallas_call | solution.py:365
  41.2 0.9 shard_map.104
  42.1 0.9 shard_map.100
  43.0 7.0 %shard_map.105 = (f32[8,128,1024]{2,1,0:T(8,128)S(1)}, f32[8,8,1024]{2,1,0:T(8,128)S(1)}, f32[8,8,1024]{2,1,0:T(8,128)S(1)}) custom-call(s32[28]{0:T(128)S(1)} %concatenate.29.sc, bf16[2,128,64,128]{3,2,1,0:T(8,128)(2,1)S(1)} %turn.1.q_ref, ...), custom_call_target="tpu_custom_call", output_to_operand_aliasing={{0}: (2, {}), {1}: (3, {}), {2}: (4, {})} | custom-call | flops 2147483648 | bytes 1048576 | tf_op jit(solution)/shard_map/pallas_call | solution.py:335
  50.0 2.5 %collective-permute-start.12 = (bf16[2,2,512,128]{3,2,1,0:T(8,128)(2,1)}, bf16[2,2,512,128]{3,2,1,0:T(8,128)(2,1)S(1)}, u32[]{:S(2)}, u32[]{:S(2)}) collective-permute-start(bf16[2,2,512,128]{3,2,1,0:T(8,128)(2,1)} %collective-permute-done.10.refs_3_), channel_id=1, source_target_pairs={{0,8},{8,16},{16,24},{24,28},{28,20},{20,12},{12,4},{4,0},{1,9},{9... | collective-permute-start | bytes 1572872 | tf_op jit(solution)/shard_map/ppermute | solution.py:443
  52.5 7.0 %shard_map.101 = (f32[8,128,1024]{2,1,0:T(8,128)S(1)}, f32[8,8,1024]{2,1,0:T(8,128)S(1)}, f32[8,8,1024]{2,1,0:T(8,128)S(1)}) custom-call(s32[28]{0:T(128)S(1)} %concatenate.29.sc, bf16[2,128,64,128]{3,2,1,0:T(8,128)(2,1)S(1)} %turn.1.q_ref, ...), custom_call_target="tpu_custom_call", output_to_operand_aliasing={{0}: (2, {}), {1}: (3, {}), {2}: (4, {})} | custom-call | flops 2147483648 | bytes 1048576 | tf_op jit(solution)/shard_map/pallas_call | solution.py:335
  59.5 6.9 %collective-permute-start.4 = (bf16[2,2,512,128]{3,2,1,0:T(8,128)(2,1)}, bf16[2,2,512,128]{3,2,1,0:T(8,128)(2,1)S(1)}, u32[]{:S(2)}, u32[]{:S(2)}) collective-permute-start(bf16[2,2,512,128]{3,2,1,0:T(8,128)(2,1)} %collective-permute-done.2.refs_3_), channel_id=1, source_target_pairs={{0,8},{8,16},{16,24},{24,28},{28,20},{20,12},{12,4},{4,0},{1,9},{9... | collective-permute-start | bytes 1572872 | tf_op jit(solution)/shard_map/ppermute | solution.py:443
  66.4 8.8 %shard_map.106 = (f32[8,128,1024]{2,1,0:T(8,128)S(1)}, f32[8,8,1024]{2,1,0:T(8,128)S(1)}, f32[8,8,1024]{2,1,0:T(8,128)S(1)}) custom-call(s32[28]{0:T(128)S(1)} %concatenate.29.sc, bf16[2,128,64,128]{3,2,1,0:T(8,128)(2,1)S(1)} %turn.1.q_ref, ...), custom_call_target="tpu_custom_call", output_to_operand_aliasing={{0}: (2, {}), {1}: (3, {}), {2}: (4, {})} | custom-call | flops 2147483648 | bytes 1048576 | tf_op jit(solution)/shard_map/pallas_call | solution.py:335
  75.2 8.8 %shard_map.102 = (f32[8,128,1024]{2,1,0:T(8,128)S(1)}, f32[8,8,1024]{2,1,0:T(8,128)S(1)}, f32[8,8,1024]{2,1,0:T(8,128)S(1)}) custom-call(s32[28]{0:T(128)S(1)} %concatenate.29.sc, bf16[2,128,64,128]{3,2,1,0:T(8,128)(2,1)S(1)} %turn.1.q_ref, ...), custom_call_target="tpu_custom_call", output_to_operand_aliasing={{0}: (2, {}), {1}: (3, {}), {2}: (4, {})} | custom-call | flops 2147483648 | bytes 1048576 | tf_op jit(solution)/shard_map/pallas_call | solution.py:335
  84.2 2.1 %collective-permute-start.15 = (bf16[2,512,128]{2,1,0:T(8,128)(2,1)S(1)}, bf16[2,512,128]{2,1,0:T(8,128)(2,1)S(1)}, u32[]{:S(2)}, u32[]{:S(2)}) collective-permute-start(bf16[2,512,128]{2,1,0:T(8,128)(2,1)S(1)} %slice_bitcast_fusion), channel_id=1, source_target_pairs={{8,0},{16,8},{24,16},{28,24},{20,28},{12,20},{4,12},{0,4},{9,1},{1... | collective-permute-start | bytes 786440 | tf_op jit(solution)/shard_map/ppermute | solution.py:443
  86.3 3.5 %collective-permute-done.5.refs_4_.refs_5_ = bf16[2,2,512,128]{3,2,1,0:T(8,128)(2,1)S(1)} collective-permute-done((bf16[2,2,512,128]{3,2,1,0:T(8,128)(2,1)S(1)}, bf16[2,2,512,128]{3,2,1,0:T(8,128)(2,1)S(1)}, u32[]{:S(2)}, u32[]{:S(2)}) %collective-permute-start.5) | collective-permute-done | bytes 524320 | tf_op jit(solution)/shard_map/ppermute | solution.py:443
  89.9 7.3 %shard_map.107 = (f32[8,128,1024]{2,1,0:T(8,128)S(1)}, f32[8,8,1024]{2,1,0:T(8,128)S(1)}, f32[8,8,1024]{2,1,0:T(8,128)S(1)}) custom-call(s32[28]{0:T(128)S(1)} %concatenate.29.sc, bf16[2,128,64,128]{3,2,1,0:T(8,128)(2,1)S(1)} %turn.1.q_ref, ...), custom_call_target="tpu_custom_call", output_to_operand_aliasing={{0}: (2, {}), {1}: (3, {}), {2}: (4, {})} | custom-call | flops 2147483648 | bytes 1048576 | tf_op jit(solution)/shard_map/pallas_call | solution.py:335
  97.2 7.5 %shard_map.103 = (f32[8,128,1024]{2,1,0:T(8,128)S(1)}, f32[8,8,1024]{2,1,0:T(8,128)S(1)}, f32[8,8,1024]{2,1,0:T(8,128)S(1)}) custom-call(s32[28]{0:T(128)S(1)} %concatenate.29.sc, bf16[2,128,64,128]{3,2,1,0:T(8,128)(2,1)S(1)} %turn.1.q_ref, ...), custom_call_target="tpu_custom_call", output_to_operand_aliasing={{0}: (2, {}), {1}: (3, {}), {2}: (4, {})} | custom-call | flops 2147483648 | bytes 1048576 | tf_op jit(solution)/shard_map/pallas_call | solution.py:335
  104.7 8.2 %shard_map.108.refs_6_ = bf16[2,128,64,128]{3,2,1,0:T(8,128)(2,1)} custom-call(s32[28]{0:T(128)S(1)} %concatenate.29.sc, bf16[2,128,64,128]{3,2,1,0:T(8,128)(2,1)S(1)} %turn.1.q_ref, f32[8,128,1024]{2,1,0:T(8,128)S(1)} %get-tuple-element.50.refs_0_, f32[8,8,1024]{2,1,0:T(8,128)S(1)} %get-tuple-element.51.refs_1_, ...), custom_call_target="tpu_custom_call" | custom-call | flops 1610612736 | bytes 1048576 | tf_op jit(solution)/shard_map/pallas_call | solution.py:335
  112.9 8.2 %shard_map.109 = bf16[2,128,64,128]{3,2,1,0:T(8,128)(2,1)} custom-call(s32[28]{0:T(128)S(1)} %concatenate.29.sc, bf16[2,128,64,128]{3,2,1,0:T(8,128)(2,1)S(1)} %turn.1.q_ref, f32[8,128,1024]{2,1,0:T(8,128)S(1)} %get-tuple-element.38.refs_0_, f32[8,8,1024]{2,1,0:T(8,128)S(1)} %get-tuple-element.39.refs_1_, ...), custom_call_target="tpu_custom_call", output_to_operand_aliasing={{}: (8, {})} | custom-call | flops 1610612736 | bytes 1048576 | tf_op jit(solution)/shard_map/pallas_call | solution.py:335
  (65 shorter events, 7.0 us)
Async XLA Ops:
  0.0 5.8 %copy-start = (bf16[2,256,4,128]{3,2,1,0:T(4,128)(2,1)S(1)}, bf16[2,256,4,128]{3,2,1,0:T(4,128)(2,1)}, u32[]{:S(2)}) copy-start(bf16[2,256,4,128]{3,2,1,0:T(4,128)(2,1)} %param.13) | copy-start | bytes 1572868
  0.0 6.0 %copy-start.1 = (bf16[2,256,4,128]{3,2,1,0:T(4,128)(2,1)S(1)}, bf16[2,256,4,128]{3,2,1,0:T(4,128)(2,1)}, u32[]{:S(2)}) copy-start(bf16[2,256,4,128]{3,2,1,0:T(4,128)(2,1)} %param.14) | copy-start | bytes 1572868
  2.2 4.2 %copy-start.2 = (bf16[2,128,4,128]{3,2,1,0:T(4,128)(2,1)S(1)}, bf16[2,128,4,128]{3,2,1,0:T(4,128)(2,1)}, u32[]{:S(2)}) copy-start(bf16[2,128,4,128]{3,2,1,0:T(4,128)(2,1)} %param.12) | copy-start | bytes 786436
  6.2 16.0 %copy-start.3 = (s32[2]{0:T(128)S(1)}, s32[2]{0:T(128)}, u32[]{:S(2)}) copy-start(s32[2]{0:T(128)} %param.15) | copy-start | bytes 28
  6.2 30.7 %copy-start.4 = (s32[2]{0:T(128)S(1)}, s32[2]{0:T(128)}, u32[]{:S(2)}) copy-start(s32[2]{0:T(128)} %param.16) | copy-start | bytes 28
  6.2 30.7 %copy-start.5 = (s32[16]{0:T(128)S(1)}, s32[16]{0:T(128)}, u32[]{:S(2)}) copy-start(s32[16]{0:T(128)} %param.18) | copy-start | bytes 196
  6.8 15.0 %collective-permute-start.8 = (bf16[2,2,512,128]{3,2,1,0:T(8,128)(2,1)S(1)}, bf16[2,2,512,128]{3,2,1,0:T(8,128)(2,1)}, u32[]{:S(2)}, u32[]{:S(2)}) collective-permute-start(bf16[2,2,512,128]{3,2,1,0:T(8,128)(2,1)S(1)} %pad_maximum_fusion.1.refs_0_.refs_3_), channel_id=1, source_target_pairs={{0,8},{8,16},{16,24},{24,28},{28,20},{20,12},{12,4},{4,0},{1,9},{9... | collective-permute-start | bytes 1572872 | tf_op jit(solution)/shard_map/ppermute | solution.py:443
  7.3 15.6 %collective-permute-start.9 = (bf16[2,2,512,128]{3,2,1,0:T(8,128)(2,1)S(1)}, bf16[2,2,512,128]{3,2,1,0:T(8,128)(2,1)S(1)}, u32[]{:S(2)}, u32[]{:S(2)}) collective-permute-start(bf16[2,2,512,128]{3,2,1,0:T(8,128)(2,1)S(1)} %pad_maximum_fusion.1.refs_0_.refs_3_), channel_id=1, source_target_pairs={{8,0},{16,8},{24,16},{28,24},{20,28},{12,20},{4,12},{0,4},{9,1},{1... | collective-permute-start | bytes 1572872 | tf_op jit(solution)/shard_map/ppermute | solution.py:443
  9.0 23.9 %collective-permute-start = (bf16[2,2,512,128]{3,2,1,0:T(8,128)(2,1)S(1)}, bf16[2,2,512,128]{3,2,1,0:T(8,128)(2,1)}, u32[]{:S(2)}, u32[]{:S(2)}) collective-permute-start(bf16[2,2,512,128]{3,2,1,0:T(8,128)(2,1)S(1)} %pad_maximum_fusion.refs_0_.refs_3_), channel_id=1, source_target_pairs={{0,8},{8,16},{16,24},{24,28},{28,20},{20,12},{12,4},{4,0},{1,9},{9... | collective-permute-start | bytes 1572872 | tf_op jit(solution)/shard_map/ppermute | solution.py:443
  9.5 23.9 %collective-permute-start.1 = (bf16[2,2,512,128]{3,2,1,0:T(8,128)(2,1)S(1)}, bf16[2,2,512,128]{3,2,1,0:T(8,128)(2,1)S(1)}, u32[]{:S(2)}, u32[]{:S(2)}) collective-permute-start(bf16[2,2,512,128]{3,2,1,0:T(8,128)(2,1)S(1)} %pad_maximum_fusion.refs_0_.refs_3_), channel_id=1, source_target_pairs={{8,0},{16,8},{24,16},{28,24},{20,28},{12,20},{4,12},{0,4},{9,1},{1... | collective-permute-start | bytes 1572872 | tf_op jit(solution)/shard_map/ppermute | solution.py:443
  21.7 28.2 %collective-permute-start.10 = (bf16[2,2,512,128]{3,2,1,0:T(8,128)(2,1)}, bf16[2,2,512,128]{3,2,1,0:T(8,128)(2,1)}, u32[]{:S(2)}, u32[]{:S(2)}) collective-permute-start(bf16[2,2,512,128]{3,2,1,0:T(8,128)(2,1)} %collective-permute-done.8.refs_4_), channel_id=1, source_target_pairs={{0,8},{8,16},{16,24},{24,28},{28,20},{20,12},{12,4},{4,0},{1,9},{9... | collective-permute-start | bytes 1572872 | tf_op jit(solution)/shard_map/ppermute | solution.py:443
  22.8 36.6 %collective-permute-start.11 = (bf16[2,2,512,128]{3,2,1,0:T(8,128)(2,1)S(1)}, bf16[2,2,512,128]{3,2,1,0:T(8,128)(2,1)S(1)}, u32[]{:S(2)}, u32[]{:S(2)}) collective-permute-start(bf16[2,2,512,128]{3,2,1,0:T(8,128)(2,1)S(1)} %collective-permute-done.9.refs_5_), channel_id=1, source_target_pairs={{8,0},{16,8},{24,16},{28,24},{20,28},{12,20},{4,12},{0,4},{9,1},{1... | collective-permute-start | bytes 1572872 | tf_op jit(solution)/shard_map/ppermute | solution.py:443
  33.0 26.6 %collective-permute-start.2 = (bf16[2,2,512,128]{3,2,1,0:T(8,128)(2,1)}, bf16[2,2,512,128]{3,2,1,0:T(8,128)(2,1)}, u32[]{:S(2)}, u32[]{:S(2)}) collective-permute-start(bf16[2,2,512,128]{3,2,1,0:T(8,128)(2,1)} %collective-permute-done.refs_4_), channel_id=1, source_target_pairs={{0,8},{8,16},{16,24},{24,28},{28,20},{20,12},{12,4},{4,0},{1,9},{9... | collective-permute-start | bytes 1572872 | tf_op jit(solution)/shard_map/ppermute | solution.py:443
  33.4 33.0 %collective-permute-start.3 = (bf16[2,2,512,128]{3,2,1,0:T(8,128)(2,1)S(1)}, bf16[2,2,512,128]{3,2,1,0:T(8,128)(2,1)S(1)}, u32[]{:S(2)}, u32[]{:S(2)}) collective-permute-start(bf16[2,2,512,128]{3,2,1,0:T(8,128)(2,1)S(1)} %collective-permute-done.1.refs_5_), channel_id=1, source_target_pairs={{8,0},{16,8},{24,16},{28,24},{20,28},{12,20},{4,12},{0,4},{9,1},{1... | collective-permute-start | bytes 1572872 | tf_op jit(solution)/shard_map/ppermute | solution.py:443
  50.0 34.0 %collective-permute-start.12 = (bf16[2,2,512,128]{3,2,1,0:T(8,128)(2,1)}, bf16[2,2,512,128]{3,2,1,0:T(8,128)(2,1)S(1)}, u32[]{:S(2)}, u32[]{:S(2)}) collective-permute-start(bf16[2,2,512,128]{3,2,1,0:T(8,128)(2,1)} %collective-permute-done.10.refs_3_), channel_id=1, source_target_pairs={{0,8},{8,16},{16,24},{24,28},{28,20},{20,12},{12,4},{4,0},{1,9},{9... | collective-permute-start | bytes 1572872 | tf_op jit(solution)/shard_map/ppermute | solution.py:443
  59.5 24.7 %collective-permute-start.13 = (bf16[2,2,512,128]{3,2,1,0:T(8,128)(2,1)S(1)}, bf16[2,2,512,128]{3,2,1,0:T(8,128)(2,1)S(1)}, u32[]{:S(2)}, u32[]{:S(2)}) collective-permute-start(bf16[2,2,512,128]{3,2,1,0:T(8,128)(2,1)S(1)} %collective-permute-done.11.refs_4_.refs_5_), channel_id=1, source_target_pairs={{8,0},{16,8},{24,16},{28,24},{20,28},{12,20},{4,12},{0,4},{9,1},{1... | collective-permute-start | bytes 1572872 | tf_op jit(solution)/shard_map/ppermute | solution.py:443
  59.5 26.7 %collective-permute-start.4 = (bf16[2,2,512,128]{3,2,1,0:T(8,128)(2,1)}, bf16[2,2,512,128]{3,2,1,0:T(8,128)(2,1)S(1)}, u32[]{:S(2)}, u32[]{:S(2)}) collective-permute-start(bf16[2,2,512,128]{3,2,1,0:T(8,128)(2,1)} %collective-permute-done.2.refs_3_), channel_id=1, source_target_pairs={{0,8},{8,16},{16,24},{24,28},{28,20},{20,12},{12,4},{4,0},{1,9},{9... | collective-permute-start | bytes 1572872 | tf_op jit(solution)/shard_map/ppermute | solution.py:443
  66.4 23.4 %collective-permute-start.5 = (bf16[2,2,512,128]{3,2,1,0:T(8,128)(2,1)S(1)}, bf16[2,2,512,128]{3,2,1,0:T(8,128)(2,1)S(1)}, u32[]{:S(2)}, u32[]{:S(2)}) collective-permute-start(bf16[2,2,512,128]{3,2,1,0:T(8,128)(2,1)S(1)} %collective-permute-done.3.refs_4_.refs_5_), channel_id=1, source_target_pairs={{8,0},{16,8},{24,16},{28,24},{20,28},{12,20},{4,12},{0,4},{9,1},{1... | collective-permute-start | bytes 1572872 | tf_op jit(solution)/shard_map/ppermute | solution.py:443
  84.0 20.6 %collective-permute-start.14 = (bf16[2,512,128]{2,1,0:T(8,128)(2,1)S(1)}, bf16[2,512,128]{2,1,0:T(8,128)(2,1)S(1)}, u32[]{:S(2)}, u32[]{:S(2)}) collective-permute-start(bf16[2,512,128]{2,1,0:T(8,128)(2,1)S(1)} %slice_bitcast_fusion.1), channel_id=1, source_target_pairs={{0,8},{8,16},{16,24},{24,28},{28,20},{20,12},{12,4},{4,0},{1,9},{9... | collective-permute-start | bytes 786440 | tf_op jit(solution)/shard_map/ppermute | solution.py:443
  84.2 20.5 %collective-permute-start.15 = (bf16[2,512,128]{2,1,0:T(8,128)(2,1)S(1)}, bf16[2,512,128]{2,1,0:T(8,128)(2,1)S(1)}, u32[]{:S(2)}, u32[]{:S(2)}) collective-permute-start(bf16[2,512,128]{2,1,0:T(8,128)(2,1)S(1)} %slice_bitcast_fusion), channel_id=1, source_target_pairs={{8,0},{16,8},{24,16},{28,24},{20,28},{12,20},{4,12},{0,4},{9,1},{1... | collective-permute-start | bytes 786440 | tf_op jit(solution)/shard_map/ppermute | solution.py:443
  86.2 26.6 %collective-permute-start.6 = (bf16[2,512,128]{2,1,0:T(8,128)(2,1)S(1)}, bf16[2,512,128]{2,1,0:T(8,128)(2,1)S(1)}, u32[]{:S(2)}, u32[]{:S(2)}) collective-permute-start(bf16[2,512,128]{2,1,0:T(8,128)(2,1)S(1)} %slice_bitcast_fusion.3), channel_id=1, source_target_pairs={{0,8},{8,16},{16,24},{24,28},{28,20},{20,12},{12,4},{4,0},{1,9},{9... | collective-permute-start | bytes 786440 | tf_op jit(solution)/shard_map/ppermute | solution.py:443
  89.8 23.1 %collective-permute-start.7 = (bf16[2,512,128]{2,1,0:T(8,128)(2,1)S(1)}, bf16[2,512,128]{2,1,0:T(8,128)(2,1)S(1)}, u32[]{:S(2)}, u32[]{:S(2)}) collective-permute-start(bf16[2,512,128]{2,1,0:T(8,128)(2,1)S(1)} %slice_bitcast_fusion.2), channel_id=1, source_target_pairs={{8,0},{16,8},{24,16},{28,24},{20,28},{12,20},{4,12},{0,4},{9,1},{1... | collective-permute-start | bytes 786440 | tf_op jit(solution)/shard_map/ppermute | solution.py:443

commit v3 on v2

--- a/solution.py
+++ b/solution.py
@@ -13,6 +13,7 @@
 log2e = 1.4426950408889634
 streams = 2
 chunk_units = 2
+lane_step = 256
 far = 1 << 29
 
 
@@ -56,28 +57,29 @@
     return x
 
 
-def largest(s, top_ref):
-    top_ref[...] = over_sublanes(jnp.maximum, jnp.max(s.reshape(-1, 8, s.shape[1]), axis=0))
-
-
-def scores(q, k, s_ref, top_ref):
+def largest(s):
+    return over_sublanes(jnp.maximum, jnp.max(s.reshape(-1, 8, s.shape[1]), axis=0))
+
+
+def scores(q, k, s_ref, top_ref, at):
     s = lax.dot_general(k, q, (((1,), (1,)), ((), ())), preferred_element_type=jnp.float32)
-    s_ref[...] = s
-    largest(s, top_ref)
-
-
-def absorb(tile, vt, s_ref, top_ref, m_ref, l_ref, acc_ref):
-    size, width = acc_ref.shape[1:]
+    s_ref[:, at] = s
+    top_ref[:, at] = largest(s)
+
+
+def absorb(tile, vt, s_ref, top_ref, m_ref, l_ref, acc_ref, at):
+    s = s_ref[:, at]
+    size, width = vt.shape[0], s.shape[1]
     factor = log2e / size**0.5
-    before = m_ref[tile]
-    top = jnp.maximum(before, top_ref[...])
+    before = m_ref[tile, :, at]
+    top = jnp.maximum(before, top_ref[:, at])
     alpha = jnp.exp2((before - top) * factor)
-    prob = jnp.exp2(s_ref[...].reshape(-1, 8, width) * factor - top * factor)
-    l_ref[tile] = l_ref[tile] * alpha + jnp.sum(prob, axis=0)
-    m_ref[tile] = top
-    prob = prob.reshape(s_ref.shape).astype(jnp.bfloat16)
-    acc = (acc_ref[tile].reshape(-1, 8, width) * alpha).reshape(size, width)
-    acc_ref[tile] = acc + jnp.dot(vt, prob, preferred_element_type=jnp.float32)
+    prob = jnp.exp2(s.reshape(-1, 8, width) * factor - top * factor)
+    l_ref[tile, :, at] = l_ref[tile, :, at] * alpha + jnp.sum(prob, axis=0)
+    m_ref[tile, :, at] = top
+    prob = prob.reshape(s.shape).astype(jnp.bfloat16)
+    acc = (acc_ref[tile, :, at].reshape(-1, 8, width) * alpha).reshape(size, width)
+    acc_ref[tile, :, at] = acc + jnp.dot(vt, prob, preferred_element_type=jnp.float32)
 
 
 def hide(token, runs, s_ref, top_ref):
@@ -221,12 +223,15 @@
         work[3, total + extra] = 0
         work[4, total + extra] = none
 
-    def prepare(at, s_ref, t_ref):
+    lanes = min(lane_step, width)
+
+    def prepare(at, s_ref, t_ref, start):
         tile = work[0, at]
         h, r, b = tile // tiles, (tile // per) % rows, tile % per
         heads_at = pl.ds(pl.multiple_of((first_head + h) * group, group), group)
-        q = q_ref[r, pl.ds(b * blk, blk), heads_at, :].reshape(width, size)
-        scores(q, kbuf[work[1, at]], s_ref, t_ref)
+        tokens_at = pl.ds(b * blk + start // group, lanes // group)
+        q = q_ref[r, tokens_at, heads_at, :].reshape(lanes, size)
+        scores(q, kbuf[work[1, at]], s_ref, t_ref, slice(start, start + lanes))
 
     def fix(at, s_ref, t_ref):
         @pl.when(work[2, at] == 1)
@@ -236,20 +241,24 @@
             table = [[work[run_at + 3 * run + j, i] for j in range(3)] for run in range(runs)]
             hide(token, table, s_ref, t_ref)
 
-    def finish(at, s_ref, t_ref):
-        absorb(work[0, at], vt_ref[work[1, at]], s_ref, t_ref, m_ref, l_ref, acc_ref)
+    def finish(at, s_ref, t_ref, start):
+        spot = slice(start, start + lanes)
+        absorb(work[0, at], vt_ref[work[1, at]], s_ref, t_ref, m_ref, l_ref, acc_ref, spot)
 
     @pl.when(total > 0)
     def _():
-        prepare(0, s0, t0)
+        for start in range(0, width, lanes):
+            prepare(0, s0, t0, start)
         fix(0, s0, t0)
 
     def body(i, _):
-        prepare(2 * i + 1, s1, t1)
-        finish(2 * i, s0, t0)
+        for start in range(0, width, lanes):
+            prepare(2 * i + 1, s1, t1, start)
+            finish(2 * i, s0, t0, start)
         fix(2 * i + 1, s1, t1)
-        prepare(2 * i + 2, s0, t0)
-        finish(2 * i + 1, s1, t1)
+        for start in range(0, width, lanes):
+            prepare(2 * i + 2, s0, t0, start)
+            finish(2 * i + 1, s1, t1, start)
         fix(2 * i + 2, s0, t0)
         return 0
 

time: 122 us -> 119 us (0.975)
  Pallas kernels: 68.6 us -> 65.4 us
  waiting for transfers between devices: 22.5 us -> 24.1 us
    pallas_call x10, Pallas kernels: 64.4 us -> 61.3 us  [step_call(): pl.pallas_call(functools.partial(step_kernel, cfg), in_specs=specs, out_s...]
    ppermute x16, waiting for transfers between devices: 22.5 us -> 24.1 us  [send(): return lax.ppermute(x, 'ctx', way)]
  transfers between devices with their start and end apart: 16 -> 16, of which waited for: 3 -> 3; matrix products, arithmetic and copies ran while one was open for 1% -> 1% of each run, Pallas kernels for 50% -> 48%
where the time goes in v3:
time: 119 us
  Pallas kernels  65.4 us (55%)
  waiting for transfers between devices  24.1 us (20%)
  starting transfers between devices  19 us (16%)
  other arithmetic  5.42 us (5%)
  between operations  2.55 us (2%)
  local copies, waits for them, and re-layouts  2.3 us (2%)
    pallas_call x10, Pallas kernels, step_call(): pl.pallas_call(functools.partial(step_kernel, cfg), in_specs=specs, out_s...  61.3 us
    ppermute x16, waiting for transfers between devices, send(): return lax.ppermute(x, 'ctx', way)  24.1 us
    ppermute x16, starting transfers between devices, send(): return lax.ppermute(x, 'ctx', way)  19 us
    pallas_call x1, Pallas kernels, turn_call(): pl.pallas_call(functools.partial(turn_kernel, parts), grid=(rows * parts,...  4.13 us
  transfers between devices with their start and end apart: 16, of which 3 were waited for; matrix products, arithmetic and copies ran while one was open for 1% of the time, Pallas kernels for 48%

profile of v3, /device:TPU:18, one launch (start us, length us, event | category | flops | bytes accessed | tf_op | source)
XLA Modules:
  0.0 118.8 jit_solution(17671946740960081463)
XLA Ops:
  0.0 0.8 dynamic-slice_multiply_fusion
  1.0 1.2 %slice_convert_fusion = (f32[2,128,2,128]{3,2,1,0:T(2,128)S(1)}, f32[2,128,2,128]{3,2,1,0:T(2,128)S(1)}) fusion(bf16[2,128,4,128]{3,2,1,0:T(4,128)(2,1)} %param.11), kind=kLoop, calls=%fused_computation.29 | loop fusion | flops 131072 | bytes 786432 | tf_op jit(solution)/shard_map/convert_element_type | solution.py:46
  3.6 0.8 subtract_convert_fusion
  7.3 1.6 %collective-permute-start.9 = (bf16[2,2,512,128]{3,2,1,0:T(8,128)(2,1)S(1)}, bf16[2,2,512,128]{3,2,1,0:T(8,128)(2,1)S(1)}, u32[]{:S(2)}, u32[]{:S(2)}) collective-permute-start(bf16[2,2,512,128]{3,2,1,0:T(8,128)(2,1)S(1)} %pad_maximum_fusion.1.refs_0_.refs_3_), channel_id=1, source_target_pairs={{8,0},{16,8},{24,16},{28,24},{20,28},{12,20},{4,12},{0,4},{9,1},{1... | collective-permute-start | bytes 1572872 | tf_op jit(solution)/shard_map/ppermute | solution.py:452
  9.5 1.6 %collective-permute-start.1 = (bf16[2,2,512,128]{3,2,1,0:T(8,128)(2,1)S(1)}, bf16[2,2,512,128]{3,2,1,0:T(8,128)(2,1)S(1)}, u32[]{:S(2)}, u32[]{:S(2)}) collective-permute-start(bf16[2,2,512,128]{3,2,1,0:T(8,128)(2,1)S(1)} %pad_maximum_fusion.refs_0_.refs_3_), channel_id=1, source_target_pairs={{8,0},{16,8},{24,16},{28,24},{20,28},{12,20},{4,12},{0,4},{9,1},{1... | collective-permute-start | bytes 1572872 | tf_op jit(solution)/shard_map/ppermute | solution.py:452
  11.2 10.5 %collective-permute-done.8.refs_4_ = bf16[2,2,512,128]{3,2,1,0:T(8,128)(2,1)} collective-permute-done((bf16[2,2,512,128]{3,2,1,0:T(8,128)(2,1)S(1)}, bf16[2,2,512,128]{3,2,1,0:T(8,128)(2,1)}, u32[]{:S(2)}, u32[]{:S(2)}) %collective-permute-start.8) | collective-permute-done | bytes 524320 | tf_op jit(solution)/shard_map/ppermute | solution.py:452
  22.8 1.6 %collective-permute-start.11 = (bf16[2,2,512,128]{3,2,1,0:T(8,128)(2,1)S(1)}, bf16[2,2,512,128]{3,2,1,0:T(8,128)(2,1)S(1)}, u32[]{:S(2)}, u32[]{:S(2)}) collective-permute-start(bf16[2,2,512,128]{3,2,1,0:T(8,128)(2,1)S(1)} %collective-permute-done.9.refs_5_), channel_id=1, source_target_pairs={{8,0},{16,8},{24,16},{28,24},{20,28},{12,20},{4,12},{0,4},{9,1},{1... | collective-permute-start | bytes 1572872 | tf_op jit(solution)/shard_map/ppermute | solution.py:452
  24.4 8.5 %collective-permute-done.refs_4_ = bf16[2,2,512,128]{3,2,1,0:T(8,128)(2,1)} collective-permute-done((bf16[2,2,512,128]{3,2,1,0:T(8,128)(2,1)S(1)}, bf16[2,2,512,128]{3,2,1,0:T(8,128)(2,1)}, u32[]{:S(2)}, u32[]{:S(2)}) %collective-permute-start) | collective-permute-done | bytes 524320 | tf_op jit(solution)/shard_map/ppermute | solution.py:452
  33.4 1.6 %collective-permute-start.3 = (bf16[2,2,512,128]{3,2,1,0:T(8,128)(2,1)S(1)}, bf16[2,2,512,128]{3,2,1,0:T(8,128)(2,1)S(1)}, u32[]{:S(2)}, u32[]{:S(2)}) collective-permute-start(bf16[2,2,512,128]{3,2,1,0:T(8,128)(2,1)S(1)} %collective-permute-done.1.refs_5_), channel_id=1, source_target_pairs={{8,0},{16,8},{24,16},{28,24},{20,28},{12,20},{4,12},{0,4},{9,1},{1... | collective-permute-start | bytes 1572872 | tf_op jit(solution)/shard_map/ppermute | solution.py:452
  37.0 4.1 %turn.1.q_ref = bf16[2,128,64,128]{3,2,1,0:T(8,128)(2,1)S(1)} custom-call(bf16[2,128,64,128]{3,2,1,0:T(8,128)(2,1)} %q_ref.1, f32[2,128,128]{2,1,0:T(8,128)S(1)} %get-tuple-element.78.cosine_ref, f32[2,128,128]{2,1,0:T(8,128)S(1)} %get-tuple-element.79.sine_ref), custom_call_target="tpu_custom_call" | custom-call | flops 8388608 | bytes 8388608 | tf_op jit(solution)/shard_map/turn/pallas_call | solution.py:374
  41.2 0.9 shard_map.104
  42.1 0.9 shard_map.100
  43.0 6.7 %shard_map.105 = (f32[8,128,1024]{2,1,0:T(8,128)S(1)}, f32[8,8,1024]{2,1,0:T(8,128)S(1)}, f32[8,8,1024]{2,1,0:T(8,128)S(1)}) custom-call(s32[28]{0:T(128)S(1)} %concatenate.29.sc, bf16[2,128,64,128]{3,2,1,0:T(8,128)(2,1)S(1)} %turn.1.q_ref, ...), custom_call_target="tpu_custom_call", output_to_operand_aliasing={{0}: (2, {}), {1}: (3, {}), {2}: (4, {})} | custom-call | flops 2147483648 | bytes 1048576 | tf_op jit(solution)/shard_map/pallas_call | solution.py:344
  49.7 2.2 %collective-permute-start.12 = (bf16[2,2,512,128]{3,2,1,0:T(8,128)(2,1)}, bf16[2,2,512,128]{3,2,1,0:T(8,128)(2,1)S(1)}, u32[]{:S(2)}, u32[]{:S(2)}) collective-permute-start(bf16[2,2,512,128]{3,2,1,0:T(8,128)(2,1)} %collective-permute-done.10.refs_3_), channel_id=1, source_target_pairs={{0,8},{8,16},{16,24},{24,28},{28,20},{20,12},{12,4},{4,0},{1,9},{9... | collective-permute-start | bytes 1572872 | tf_op jit(solution)/shard_map/ppermute | solution.py:452
  51.8 6.8 %shard_map.101 = (f32[8,128,1024]{2,1,0:T(8,128)S(1)}, f32[8,8,1024]{2,1,0:T(8,128)S(1)}, f32[8,8,1024]{2,1,0:T(8,128)S(1)}) custom-call(s32[28]{0:T(128)S(1)} %concatenate.29.sc, bf16[2,128,64,128]{3,2,1,0:T(8,128)(2,1)S(1)} %turn.1.q_ref, ...), custom_call_target="tpu_custom_call", output_to_operand_aliasing={{0}: (2, {}), {1}: (3, {}), {2}: (4, {})} | custom-call | flops 2147483648 | bytes 1048576 | tf_op jit(solution)/shard_map/pallas_call | solution.py:344
  58.7 6.3 %collective-permute-start.4 = (bf16[2,2,512,128]{3,2,1,0:T(8,128)(2,1)}, bf16[2,2,512,128]{3,2,1,0:T(8,128)(2,1)S(1)}, u32[]{:S(2)}, u32[]{:S(2)}) collective-permute-start(bf16[2,2,512,128]{3,2,1,0:T(8,128)(2,1)} %collective-permute-done.2.refs_3_), channel_id=1, source_target_pairs={{0,8},{8,16},{16,24},{24,28},{28,20},{20,12},{12,4},{4,0},{1,9},{9... | collective-permute-start | bytes 1572872 | tf_op jit(solution)/shard_map/ppermute | solution.py:452
  65.1 8.3 %shard_map.106 = (f32[8,128,1024]{2,1,0:T(8,128)S(1)}, f32[8,8,1024]{2,1,0:T(8,128)S(1)}, f32[8,8,1024]{2,1,0:T(8,128)S(1)}) custom-call(s32[28]{0:T(128)S(1)} %concatenate.29.sc, bf16[2,128,64,128]{3,2,1,0:T(8,128)(2,1)S(1)} %turn.1.q_ref, ...), custom_call_target="tpu_custom_call", output_to_operand_aliasing={{0}: (2, {}), {1}: (3, {}), {2}: (4, {})} | custom-call | flops 2147483648 | bytes 1048576 | tf_op jit(solution)/shard_map/pallas_call | solution.py:344
  73.4 8.3 %shard_map.102 = (f32[8,128,1024]{2,1,0:T(8,128)S(1)}, f32[8,8,1024]{2,1,0:T(8,128)S(1)}, f32[8,8,1024]{2,1,0:T(8,128)S(1)}) custom-call(s32[28]{0:T(128)S(1)} %concatenate.29.sc, bf16[2,128,64,128]{3,2,1,0:T(8,128)(2,1)S(1)} %turn.1.q_ref, ...), custom_call_target="tpu_custom_call", output_to_operand_aliasing={{0}: (2, {}), {1}: (3, {}), {2}: (4, {})} | custom-call | flops 2147483648 | bytes 1048576 | tf_op jit(solution)/shard_map/pallas_call | solution.py:344
  81.8 2.1 %collective-permute-start.15 = (bf16[2,512,128]{2,1,0:T(8,128)(2,1)S(1)}, bf16[2,512,128]{2,1,0:T(8,128)(2,1)S(1)}, u32[]{:S(2)}, u32[]{:S(2)}) collective-permute-start(bf16[2,512,128]{2,1,0:T(8,128)(2,1)S(1)} %slice_bitcast_fusion), channel_id=1, source_target_pairs={{8,0},{16,8},{24,16},{28,24},{20,28},{12,20},{4,12},{0,4},{9,1},{1... | collective-permute-start | bytes 786440 | tf_op jit(solution)/shard_map/ppermute | solution.py:452
  84.0 5.0 %collective-permute-done.5.refs_4_.refs_5_ = bf16[2,2,512,128]{3,2,1,0:T(8,128)(2,1)S(1)} collective-permute-done((bf16[2,2,512,128]{3,2,1,0:T(8,128)(2,1)S(1)}, bf16[2,2,512,128]{3,2,1,0:T(8,128)(2,1)S(1)}, u32[]{:S(2)}, u32[]{:S(2)}) %collective-permute-start.5) | collective-permute-done | bytes 524320 | tf_op jit(solution)/shard_map/ppermute | solution.py:452
  89.1 6.8 %shard_map.107 = (f32[8,128,1024]{2,1,0:T(8,128)S(1)}, f32[8,8,1024]{2,1,0:T(8,128)S(1)}, f32[8,8,1024]{2,1,0:T(8,128)S(1)}) custom-call(s32[28]{0:T(128)S(1)} %concatenate.29.sc, bf16[2,128,64,128]{3,2,1,0:T(8,128)(2,1)S(1)} %turn.1.q_ref, ...), custom_call_target="tpu_custom_call", output_to_operand_aliasing={{0}: (2, {}), {1}: (3, {}), {2}: (4, {})} | custom-call | flops 2147483648 | bytes 1048576 | tf_op jit(solution)/shard_map/pallas_call | solution.py:344
  95.9 6.8 %shard_map.103 = (f32[8,128,1024]{2,1,0:T(8,128)S(1)}, f32[8,8,1024]{2,1,0:T(8,128)S(1)}, f32[8,8,1024]{2,1,0:T(8,128)S(1)}) custom-call(s32[28]{0:T(128)S(1)} %concatenate.29.sc, bf16[2,128,64,128]{3,2,1,0:T(8,128)(2,1)S(1)} %turn.1.q_ref, ...), custom_call_target="tpu_custom_call", output_to_operand_aliasing={{0}: (2, {}), {1}: (3, {}), {2}: (4, {})} | custom-call | flops 2147483648 | bytes 1048576 | tf_op jit(solution)/shard_map/pallas_call | solution.py:344
  102.7 8.1 %shard_map.108.refs_6_ = bf16[2,128,64,128]{3,2,1,0:T(8,128)(2,1)} custom-call(s32[28]{0:T(128)S(1)} %concatenate.29.sc, bf16[2,128,64,128]{3,2,1,0:T(8,128)(2,1)S(1)} %turn.1.q_ref, f32[8,128,1024]{2,1,0:T(8,128)S(1)} %get-tuple-element.50.refs_0_, f32[8,8,1024]{2,1,0:T(8,128)S(1)} %get-tuple-element.51.refs_1_, ...), custom_call_target="tpu_custom_call" | custom-call | flops 1610612736 | bytes 1048576 | tf_op jit(solution)/shard_map/pallas_call | solution.py:344
  110.8 7.8 %shard_map.109 = bf16[2,128,64,128]{3,2,1,0:T(8,128)(2,1)} custom-call(s32[28]{0:T(128)S(1)} %concatenate.29.sc, bf16[2,128,64,128]{3,2,1,0:T(8,128)(2,1)S(1)} %turn.1.q_ref, f32[8,128,1024]{2,1,0:T(8,128)S(1)} %get-tuple-element.38.refs_0_, f32[8,8,1024]{2,1,0:T(8,128)S(1)} %get-tuple-element.39.refs_1_, ...), custom_call_target="tpu_custom_call", output_to_operand_aliasing={{}: (8, {})} | custom-call | flops 1610612736 | bytes 1048576 | tf_op jit(solution)/shard_map/pallas_call | solution.py:344
  (65 shorter events, 7.0 us)
Async XLA Ops:
  0.0 5.8 %copy-start = (bf16[2,256,4,128]{3,2,1,0:T(4,128)(2,1)S(1)}, bf16[2,256,4,128]{3,2,1,0:T(4,128)(2,1)}, u32[]{:S(2)}) copy-start(bf16[2,256,4,128]{3,2,1,0:T(4,128)(2,1)} %param.13) | copy-start | bytes 1572868
  0.0 6.0 %copy-start.1 = (bf16[2,256,4,128]{3,2,1,0:T(4,128)(2,1)S(1)}, bf16[2,256,4,128]{3,2,1,0:T(4,128)(2,1)}, u32[]{:S(2)}) copy-start(bf16[2,256,4,128]{3,2,1,0:T(4,128)(2,1)} %param.14) | copy-start | bytes 1572868
  2.2 4.2 %copy-start.2 = (bf16[2,128,4,128]{3,2,1,0:T(4,128)(2,1)S(1)}, bf16[2,128,4,128]{3,2,1,0:T(4,128)(2,1)}, u32[]{:S(2)}) copy-start(bf16[2,128,4,128]{3,2,1,0:T(4,128)(2,1)} %param.12) | copy-start | bytes 786436
  6.2 16.0 %copy-start.3 = (s32[2]{0:T(128)S(1)}, s32[2]{0:T(128)}, u32[]{:S(2)}) copy-start(s32[2]{0:T(128)} %param.15) | copy-start | bytes 28
  6.2 30.7 %copy-start.4 = (s32[2]{0:T(128)S(1)}, s32[2]{0:T(128)}, u32[]{:S(2)}) copy-start(s32[2]{0:T(128)} %param.16) | copy-start | bytes 28
  6.2 30.7 %copy-start.5 = (s32[16]{0:T(128)S(1)}, s32[16]{0:T(128)}, u32[]{:S(2)}) copy-start(s32[16]{0:T(128)} %param.18) | copy-start | bytes 196
  6.8 15.0 %collective-permute-start.8 = (bf16[2,2,512,128]{3,2,1,0:T(8,128)(2,1)S(1)}, bf16[2,2,512,128]{3,2,1,0:T(8,128)(2,1)}, u32[]{:S(2)}, u32[]{:S(2)}) collective-permute-start(bf16[2,2,512,128]{3,2,1,0:T(8,128)(2,1)S(1)} %pad_maximum_fusion.1.refs_0_.refs_3_), channel_id=1, source_target_pairs={{0,8},{8,16},{16,24},{24,28},{28,20},{20,12},{12,4},{4,0},{1,9},{9... | collective-permute-start | bytes 1572872 | tf_op jit(solution)/shard_map/ppermute | solution.py:452
  7.3 15.6 %collective-permute-start.9 = (bf16[2,2,512,128]{3,2,1,0:T(8,128)(2,1)S(1)}, bf16[2,2,512,128]{3,2,1,0:T(8,128)(2,1)S(1)}, u32[]{:S(2)}, u32[]{:S(2)}) collective-permute-start(bf16[2,2,512,128]{3,2,1,0:T(8,128)(2,1)S(1)} %pad_maximum_fusion.1.refs_0_.refs_3_), channel_id=1, source_target_pairs={{8,0},{16,8},{24,16},{28,24},{20,28},{12,20},{4,12},{0,4},{9,1},{1... | collective-permute-start | bytes 1572872 | tf_op jit(solution)/shard_map/ppermute | solution.py:452
  9.0 23.9 %collective-permute-start = (bf16[2,2,512,128]{3,2,1,0:T(8,128)(2,1)S(1)}, bf16[2,2,512,128]{3,2,1,0:T(8,128)(2,1)}, u32[]{:S(2)}, u32[]{:S(2)}) collective-permute-start(bf16[2,2,512,128]{3,2,1,0:T(8,128)(2,1)S(1)} %pad_maximum_fusion.refs_0_.refs_3_), channel_id=1, source_target_pairs={{0,8},{8,16},{16,24},{24,28},{28,20},{20,12},{12,4},{4,0},{1,9},{9... | collective-permute-start | bytes 1572872 | tf_op jit(solution)/shard_map/ppermute | solution.py:452
  9.5 23.9 %collective-permute-start.1 = (bf16[2,2,512,128]{3,2,1,0:T(8,128)(2,1)S(1)}, bf16[2,2,512,128]{3,2,1,0:T(8,128)(2,1)S(1)}, u32[]{:S(2)}, u32[]{:S(2)}) collective-permute-start(bf16[2,2,512,128]{3,2,1,0:T(8,128)(2,1)S(1)} %pad_maximum_fusion.refs_0_.refs_3_), channel_id=1, source_target_pairs={{8,0},{16,8},{24,16},{28,24},{20,28},{12,20},{4,12},{0,4},{9,1},{1... | collective-permute-start | bytes 1572872 | tf_op jit(solution)/shard_map/ppermute | solution.py:452
  21.7 27.9 %collective-permute-start.10 = (bf16[2,2,512,128]{3,2,1,0:T(8,128)(2,1)}, bf16[2,2,512,128]{3,2,1,0:T(8,128)(2,1)}, u32[]{:S(2)}, u32[]{:S(2)}) collective-permute-start(bf16[2,2,512,128]{3,2,1,0:T(8,128)(2,1)} %collective-permute-done.8.refs_4_), channel_id=1, source_target_pairs={{0,8},{8,16},{16,24},{24,28},{28,20},{20,12},{12,4},{4,0},{1,9},{9... | collective-permute-start | bytes 1572872 | tf_op jit(solution)/shard_map/ppermute | solution.py:452
  22.8 35.8 %collective-permute-start.11 = (bf16[2,2,512,128]{3,2,1,0:T(8,128)(2,1)S(1)}, bf16[2,2,512,128]{3,2,1,0:T(8,128)(2,1)S(1)}, u32[]{:S(2)}, u32[]{:S(2)}) collective-permute-start(bf16[2,2,512,128]{3,2,1,0:T(8,128)(2,1)S(1)} %collective-permute-done.9.refs_5_), channel_id=1, source_target_pairs={{8,0},{16,8},{24,16},{28,24},{20,28},{12,20},{4,12},{0,4},{9,1},{1... | collective-permute-start | bytes 1572872 | tf_op jit(solution)/shard_map/ppermute | solution.py:452
  33.0 25.7 %collective-permute-start.2 = (bf16[2,2,512,128]{3,2,1,0:T(8,128)(2,1)}, bf16[2,2,512,128]{3,2,1,0:T(8,128)(2,1)}, u32[]{:S(2)}, u32[]{:S(2)}) collective-permute-start(bf16[2,2,512,128]{3,2,1,0:T(8,128)(2,1)} %collective-permute-done.refs_4_), channel_id=1, source_target_pairs={{0,8},{8,16},{16,24},{24,28},{28,20},{20,12},{12,4},{4,0},{1,9},{9... | collective-permute-start | bytes 1572872 | tf_op jit(solution)/shard_map/ppermute | solution.py:452
  33.4 31.7 %collective-permute-start.3 = (bf16[2,2,512,128]{3,2,1,0:T(8,128)(2,1)S(1)}, bf16[2,2,512,128]{3,2,1,0:T(8,128)(2,1)S(1)}, u32[]{:S(2)}, u32[]{:S(2)}) collective-permute-start(bf16[2,2,512,128]{3,2,1,0:T(8,128)(2,1)S(1)} %collective-permute-done.1.refs_5_), channel_id=1, source_target_pairs={{8,0},{16,8},{24,16},{28,24},{20,28},{12,20},{4,12},{0,4},{9,1},{1... | collective-permute-start | bytes 1572872 | tf_op jit(solution)/shard_map/ppermute | solution.py:452
  49.7 32.0 %collective-permute-start.12 = (bf16[2,2,512,128]{3,2,1,0:T(8,128)(2,1)}, bf16[2,2,512,128]{3,2,1,0:T(8,128)(2,1)S(1)}, u32[]{:S(2)}, u32[]{:S(2)}) collective-permute-start(bf16[2,2,512,128]{3,2,1,0:T(8,128)(2,1)} %collective-permute-done.10.refs_3_), channel_id=1, source_target_pairs={{0,8},{8,16},{16,24},{24,28},{28,20},{20,12},{12,4},{4,0},{1,9},{9... | collective-permute-start | bytes 1572872 | tf_op jit(solution)/shard_map/ppermute | solution.py:452
  58.6 23.1 %collective-permute-start.13 = (bf16[2,2,512,128]{3,2,1,0:T(8,128)(2,1)S(1)}, bf16[2,2,512,128]{3,2,1,0:T(8,128)(2,1)S(1)}, u32[]{:S(2)}, u32[]{:S(2)}) collective-permute-start(bf16[2,2,512,128]{3,2,1,0:T(8,128)(2,1)S(1)} %collective-permute-done.11.refs_4_.refs_5_), channel_id=1, source_target_pairs={{8,0},{16,8},{24,16},{28,24},{20,28},{12,20},{4,12},{0,4},{9,1},{1... | collective-permute-start | bytes 1572872 | tf_op jit(solution)/shard_map/ppermute | solution.py:452
  58.7 25.2 %collective-permute-start.4 = (bf16[2,2,512,128]{3,2,1,0:T(8,128)(2,1)}, bf16[2,2,512,128]{3,2,1,0:T(8,128)(2,1)S(1)}, u32[]{:S(2)}, u32[]{:S(2)}) collective-permute-start(bf16[2,2,512,128]{3,2,1,0:T(8,128)(2,1)} %collective-permute-done.2.refs_3_), channel_id=1, source_target_pairs={{0,8},{8,16},{16,24},{24,28},{28,20},{20,12},{12,4},{4,0},{1,9},{9... | collective-permute-start | bytes 1572872 | tf_op jit(solution)/shard_map/ppermute | solution.py:452
  65.1 23.9 %collective-permute-start.5 = (bf16[2,2,512,128]{3,2,1,0:T(8,128)(2,1)S(1)}, bf16[2,2,512,128]{3,2,1,0:T(8,128)(2,1)S(1)}, u32[]{:S(2)}, u32[]{:S(2)}) collective-permute-start(bf16[2,2,512,128]{3,2,1,0:T(8,128)(2,1)S(1)} %collective-permute-done.3.refs_4_.refs_5_), channel_id=1, source_target_pairs={{8,0},{16,8},{24,16},{28,24},{20,28},{12,20},{4,12},{0,4},{9,1},{1... | collective-permute-start | bytes 1572872 | tf_op jit(solution)/shard_map/ppermute | solution.py:452
  81.7 21.0 %collective-permute-start.14 = (bf16[2,512,128]{2,1,0:T(8,128)(2,1)S(1)}, bf16[2,512,128]{2,1,0:T(8,128)(2,1)S(1)}, u32[]{:S(2)}, u32[]{:S(2)}) collective-permute-start(bf16[2,512,128]{2,1,0:T(8,128)(2,1)S(1)} %slice_bitcast_fusion.1), channel_id=1, source_target_pairs={{0,8},{8,16},{16,24},{24,28},{28,20},{20,12},{12,4},{4,0},{1,9},{9... | collective-permute-start | bytes 786440 | tf_op jit(solution)/shard_map/ppermute | solution.py:452
  81.8 20.9 %collective-permute-start.15 = (bf16[2,512,128]{2,1,0:T(8,128)(2,1)S(1)}, bf16[2,512,128]{2,1,0:T(8,128)(2,1)S(1)}, u32[]{:S(2)}, u32[]{:S(2)}) collective-permute-start(bf16[2,512,128]{2,1,0:T(8,128)(2,1)S(1)} %slice_bitcast_fusion), channel_id=1, source_target_pairs={{8,0},{16,8},{24,16},{28,24},{20,28},{12,20},{4,12},{0,4},{9,1},{1... | collective-permute-start | bytes 786440 | tf_op jit(solution)/shard_map/ppermute | solution.py:452
  83.9 26.9 %collective-permute-start.6 = (bf16[2,512,128]{2,1,0:T(8,128)(2,1)S(1)}, bf16[2,512,128]{2,1,0:T(8,128)(2,1)S(1)}, u32[]{:S(2)}, u32[]{:S(2)}) collective-permute-start(bf16[2,512,128]{2,1,0:T(8,128)(2,1)S(1)} %slice_bitcast_fusion.3), channel_id=1, source_target_pairs={{0,8},{8,16},{16,24},{24,28},{28,20},{20,12},{12,4},{4,0},{1,9},{9... | collective-permute-start | bytes 786440 | tf_op jit(solution)/shard_map/ppermute | solution.py:452
  89.0 21.8 %collective-permute-start.7 = (bf16[2,512,128]{2,1,0:T(8,128)(2,1)S(1)}, bf16[2,512,128]{2,1,0:T(8,128)(2,1)S(1)}, u32[]{:S(2)}, u32[]{:S(2)}) collective-permute-start(bf16[2,512,128]{2,1,0:T(8,128)(2,1)S(1)} %slice_bitcast_fusion.2), channel_id=1, source_target_pairs={{8,0},{16,8},{24,16},{28,24},{20,28},{12,20},{4,12},{0,4},{9,1},{1... | collective-permute-start | bytes 786440 | tf_op jit(solution)/shard_map/ppermute | solution.py:452
